TPU v7x, 512 devices: a whole 4x4x16 slice. The times are simulated.
512 devices in a mesh: req: 64 (over x, z), head: 8 (over y, core).
Axes of the slice: x: 4, y: 4, z: 16, core: 2. Of those that a mesh axis runs over, the one named last changes fastest.
Arguments:
- guessed_symbol_features: bfloat16 [512, 16, 2048], P('req', None, 'head'), may hold values from -6 to 6
- earlier_feature: bfloat16 [512, 2048], P('req', 'head'), may hold values from -6 to 6
- query_memory_summary: float32 [512, 16, 64, 64], P('req', 'head'), may hold values from -6 to 6
- approved_guesses: int32 [512], P('req'), may hold values from 0 to 16
- query_ordinals: int32 [512], P('req'), may hold values from 0 to 511, as said below
- restored_ordinals: int32 [64], P('req'), may hold values from 0 to 511, as said below
- symbols_following_snapshot: int32 [64], P('req'), may hold values from 1 to 32, as said below
- snapshot_summaries: float32 [64, 16, 64, 64], P('req', 'head'), may hold values from -6 to 6
- following_snapshot_features: bfloat16 [64, 32, 2048], P('req', None, 'head'), may hold values from -6 to 6
- earlier_segment_feature: bfloat16 [64, 2048], P('req', 'head'), may hold values from -6 to 6
- acceptor_coefficients: bfloat16 [2048, 1024], P(None, 'head'), may hold values from -0.125 to 0.125
- address_coefficients: bfloat16 [2048, 1024], P(None, 'head'), may hold values from -0.125 to 0.125
- payload_coefficients: bfloat16 [2048, 1024], P(None, 'head'), may hold values from -0.125 to 0.125
- lagged_interpolants: float32 [4, 2048], replicated, may hold values from 0 to 1
- fading_narrowing_matrix: bfloat16 [2048, 64], replicated, may hold values from -0.125 to 0.125
- fading_expanding_matrix: bfloat16 [64, 1024], P(None, 'head'), may hold values from -0.75 to 0.75
- lane_fading_logit: float32 [1024], P('head'), may hold values from -6 to -1
- present_step_reward: float32 [1024], P('head'), may hold values from -3 to 3
- cluster_scaling_vector: float32 [1024], P('head'), may hold values from 0.1 to 1.9
Outputs:
- verified: bfloat16 [512, 16, 1024], P('req', None, 'head')
- new_state: float32 [512, 16, 64, 64], P('req', 'head')
Inputs may be any that keep to these rules, and one draw needn't show every extreme that they name: `query_ordinals`: a permutation of 0..511; request r belongs to device query_ordinals[r] // 8 of req in the balanced order. The 8 requests held on one req device belong to 8 distinct req devices in the balanced order, and each req device has 8 requests belonging to it, held on 8 distinct req devices. `restored_ordinals`: Distinct; entry j lies between (j) * 8 and (j + 1) * 8 - 1. `symbols_following_snapshot`: some entry equals 32 in every draw.
All inputs are finite; a program needn't handle non-finite values.
Results may differ from a plain program's by a relative error of at most 0.0061.
Values may be sent and summed in bfloat16 or wider, within the bound.
A program may use at most 64 MiB of HBM per device.

v0:
```python
import jax
import jax.numpy as jnp
from jax import lax
from jax.sharding import PartitionSpec as P

PARTITION_LENGTH = 64


NORM_EPS = 0.00064


def mixed_inputs(token_inputs, prior_state, lagged_interpolants):
    shifted = jnp.concatenate([prior_state[:, None, :], token_inputs[:, :-1, :]], axis=1)
    present_step = token_inputs.astype(jnp.float32)
    change = shifted.astype(jnp.float32) - present_step
    return [
        (present_step + change * lagged_interpolants[position]).astype(jnp.bfloat16)
        for position in range(4)
    ]


def projection_weights(
    token_inputs,
    prior_state,
    receptance_gated_output,
    lagged_interpolants,
    acceptor_coefficients,
    address_coefficients,
    payload_coefficients,
    fading_narrowing_matrix,
    fading_expanding_matrix,
    lane_fading_logit,
):
    number, length, features = token_inputs.shape
    shift_blended = [
        member.reshape(number * length, features)
        for member in mixed_inputs(token_inputs, prior_state, lagged_interpolants)
    ]
    address_mapped = jnp.dot(
        shift_blended[1], address_coefficients, preferred_element_type=jnp.float32
    )
    payload_mapped = jnp.dot(
        shift_blended[2], payload_coefficients, preferred_element_type=jnp.float32
    )
    decay_lowrank_term = jnp.tanh(
        jnp.dot(shift_blended[3], fading_narrowing_matrix, preferred_element_type=jnp.float32)
    ).astype(jnp.bfloat16)
    fading_multiplier = jnp.exp(
        -jnp.exp(
            lane_fading_logit
            + jnp.dot(
                decay_lowrank_term, fading_expanding_matrix, preferred_element_type=jnp.float32
            )
        )
    )
    results = [address_mapped, payload_mapped, fading_multiplier]
    if receptance_gated_output:
        results = [
            jnp.dot(shift_blended[0], acceptor_coefficients, preferred_element_type=jnp.float32)
        ] + results
    return tuple((member.reshape(number, length, -1, PARTITION_LENGTH) for member in results))


def advance(initial_summary, address_mapped, payload_mapped, fading_multiplier, valid_mask):

    def advance_update(running, inputs):
        present_address, present_payload, decay_now, valid_now = inputs
        advanced = (
            decay_now[..., :, None] * running
            + present_address[..., :, None] * present_payload[..., None, :]
        )
        return (jnp.where(valid_now[:, None, None, None], advanced, running), None)

    series = tuple(
        (
            jnp.moveaxis(member, 1, 0)
            for member in (address_mapped, payload_mapped, fading_multiplier, valid_mask)
        )
    )
    finished, _ = lax.scan(advance_update, initial_summary, series)
    return finished


def confirm_guesses(
    initial_summary,
    acceptor_lines,
    address_mapped,
    payload_mapped,
    fading_multiplier,
    present_step_reward,
    approved_guesses,
):
    reward_for_partition = present_step_reward.reshape(-1, PARTITION_LENGTH)[None]

    def confirm_update(running, inputs):
        present_step, chosen_summary = running
        present_acceptor, present_address, present_payload, decay_now, position = inputs
        readout_vector = jnp.einsum(
            "nhi,nhij->nhj", present_acceptor, present_step, precision=lax.Precision.HIGHEST
        )
        immediate_reward_part = (
            jnp.sum(
                present_acceptor * reward_for_partition * present_address, axis=-1, keepdims=True
            )
            * present_payload
        )
        present_step = (
            decay_now[..., :, None] * present_step
            + present_address[..., :, None] * present_payload[..., None, :]
        )
        chosen_summary = jnp.where(
            (approved_guesses > position)[:, None, None, None], present_step, chosen_summary
        )
        return ((present_step, chosen_summary), readout_vector + immediate_reward_part)

    positions = jnp.arange(acceptor_lines.shape[1], dtype=jnp.int32)
    series = tuple(
        (
            jnp.moveaxis(member, 1, 0)
            for member in (acceptor_lines, address_mapped, payload_mapped, fading_multiplier)
        )
    ) + (positions,)
    (_, chosen_summary), sublevel_results = lax.scan(
        confirm_update, (initial_summary, initial_summary), series
    )
    return (chosen_summary, jnp.moveaxis(sublevel_results, 0, 1))


def group_norm(sublevel_results, cluster_scaling_vector):
    centre = sublevel_results - jnp.mean(sublevel_results, axis=-1, keepdims=True)
    spread = jnp.mean(centre * centre, axis=-1, keepdims=True)
    normed = centre * lax.rsqrt(spread + NORM_EPS)
    flat = normed.reshape(normed.shape[0], normed.shape[1], -1)
    return (flat * cluster_scaling_vector).astype(jnp.bfloat16)


def widen(
    guessed_symbol_features, earlier_feature, following_snapshot_features, earlier_segment_feature
):
    widened_drafts, widened_preceding, wide_span, wide_span_prev = (
        lax.all_gather(guessed_symbol_features, "head", axis=2, tiled=True),
        lax.all_gather(earlier_feature[:, None, :], "head", axis=2, tiled=True),
        lax.all_gather(following_snapshot_features, "head", axis=2, tiled=True),
        lax.all_gather(earlier_segment_feature[:, None, :], "head", axis=2, tiled=True),
    )
    return (widened_drafts, widened_preceding[:, 0, :], wide_span, wide_span_prev[:, 0, :])


def rebuild(
    wide_span, wide_span_prev, symbols_following_snapshot, snapshot_summaries, layer_weights
):
    span_key, span_value, span_decay = projection_weights(
        wide_span, wide_span_prev, False, *layer_weights
    )
    valid_mask = (
        jnp.arange(wide_span.shape[1], dtype=jnp.int32)[None, :]
        < symbols_following_snapshot[:, None]
    )
    return advance(snapshot_summaries, span_key, span_value, span_decay, valid_mask)


def apply_mixing_layer(
    initial_summary,
    widened_drafts,
    widened_preceding,
    layer_weights,
    present_step_reward,
    cluster_scaling_vector,
    approved_guesses,
):
    acceptor_lines, address_mapped, payload_mapped, fading_multiplier = projection_weights(
        widened_drafts, widened_preceding, True, *layer_weights
    )
    chosen_summary, sublevel_results = confirm_guesses(
        initial_summary,
        acceptor_lines,
        address_mapped,
        payload_mapped,
        fading_multiplier,
        present_step_reward,
        approved_guesses,
    )
    return (chosen_summary, group_norm(sublevel_results, cluster_scaling_vector))


def entry_of(matched):
    picked = jnp.sum(
        jnp.where(matched, jnp.arange(matched.shape[1], dtype=jnp.int32)[None, :], 0), axis=1
    )
    return (picked, jnp.any(matched, axis=1))


def per_device(
    guessed_symbol_features,
    earlier_feature,
    query_memory_summary,
    approved_guesses,
    query_ordinals,
    restored_ordinals,
    symbols_following_snapshot,
    snapshot_summaries,
    following_snapshot_features,
    earlier_segment_feature,
    acceptor_coefficients,
    address_coefficients,
    payload_coefficients,
    lagged_interpolants,
    fading_narrowing_matrix,
    fading_expanding_matrix,
    lane_fading_logit,
    present_step_reward,
    cluster_scaling_vector,
):
    layer_weights = (
        lagged_interpolants,
        acceptor_coefficients,
        address_coefficients,
        payload_coefficients,
        fading_narrowing_matrix,
        fading_expanding_matrix,
        lane_fading_logit,
    )
    widened_drafts, widened_preceding, wide_span, wide_span_prev = widen(
        guessed_symbol_features,
        earlier_feature,
        following_snapshot_features,
        earlier_segment_feature,
    )
    rebuilt_states = rebuild(
        wide_span, wide_span_prev, symbols_following_snapshot, snapshot_summaries, layer_weights
    )
    slot_values = restored_ordinals.astype(jnp.float32)
    wanted = query_ordinals.astype(jnp.float32)
    states_piece = lax.all_gather(rebuilt_states, "req", axis=0, tiled=True)
    slots_piece = lax.all_gather(slot_values, "req", axis=0, tiled=True)
    which_entry, has_rebuild = entry_of(wanted[:, None] == slots_piece[None, :])
    initial_summary = jnp.where(
        has_rebuild[:, None, None, None],
        jnp.take(states_piece, which_entry, axis=0),
        query_memory_summary,
    )
    result_state, result_rows = apply_mixing_layer(
        initial_summary,
        widened_drafts,
        widened_preceding,
        layer_weights,
        present_step_reward,
        cluster_scaling_vector,
        approved_guesses,
    )
    return (result_rows, result_state)


def solution(mesh):
    in_specs = (
        P("req", None, "head"),
        P("req", "head"),
        P("req", "head", None, None),
        P("req"),
        P("req"),
        P("req"),
        P("req"),
        P("req", "head", None, None),
        P("req", None, "head"),
        P("req", "head"),
        P(None, "head"),
        P(None, "head"),
        P(None, "head"),
        P(),
        P(),
        P(None, "head"),
        P("head"),
        P("head"),
        P("head"),
    )
    out_specs = (P("req", None, "head"), P("req", "head", None, None))
    return jax.shard_map(
        per_device, mesh=mesh, in_specs=in_specs, out_specs=out_specs, check_vma=False
    )
```

profile of v0, /device:TPU:24, one launch (start us, length us, event | category | flops | bytes accessed | tf_op | source)
XLA Modules:
  0.0 312.2 jit_solution(15507169653192960407)
XLA Ops:
  7.3 15.6 %all_gather.19 = bf16[1,32,2048]{2,1,0:T(8,128)(2,1)S(1)} all-gather(bf16[1,32,256]{2,1,0:T(8,128)(2,1)} %param.31), channel_id=1, replica_groups=mesh['req'=64,'head'=8] {'head'}, dimensions={2}, use_global_device_ids=true | all-gather | bytes 147456 | tf_op jit(solution)/shard_map/all_gather | solution.py:143
  22.9 0.9 fusion.51
  23.8 10.0 %all-gather = bf16[1,2048]{1,0:T(2,128)(2,1)S(1)} all-gather(bf16[1,256]{1,0:T(2,128)(2,1)} %param.32), channel_id=2, replica_groups=mesh['req'=64,'head'=8] {'head'}, dimensions={1}, use_global_device_ids=true | all-gather | bytes 4608 | tf_op jit(solution)/shard_map/all_gather | solution.py:144
  33.8 1.2 copy.60
  35.0 1.3 copy.59
  36.4 1.1 fusion.14
  38.9 42.1 %while.24 = (s32[]{:T(128)}, f32[1,2,64,64]{3,2,1,0:T(8,128)S(1)}, pred[32,1]{0,1:T(4,128)(4,1)S(1)}, f32[32,1,2,64]{3,2,1,0:T(2,128)S(1)}, f32[32,1,2,64]{3,0,2...) while((s32[]{:T(128)}, f32[1,2,64,64]{3,2,1,0:T(8,128)S(1)}, pred[32,1]{0,1:T(4,128)(4,1)S(1)}, ...), condition=%wide.region_3.4_spmd, body=%wide.region_2.3_spmd.sunk | while | flops 32770 | bytes 70236 | solution.py:80
  39.6 0.7 add_select_fusion.2
  40.9 0.7 add_select_fusion.2
  42.2 0.7 add_select_fusion.2
  43.5 0.7 add_select_fusion.2
  44.8 0.7 add_select_fusion.2
  46.1 0.7 add_select_fusion.2
  47.5 0.7 add_select_fusion.2
  48.8 0.7 add_select_fusion.2
  50.1 0.7 add_select_fusion.2
  51.4 0.7 add_select_fusion.2
  52.7 0.7 add_select_fusion.2
  54.0 0.7 add_select_fusion.2
  55.4 0.7 add_select_fusion.2
  56.7 0.7 add_select_fusion.2
  58.0 0.7 add_select_fusion.2
  59.3 0.7 add_select_fusion.2
  60.6 0.7 add_select_fusion.2
  61.9 0.7 add_select_fusion.2
  63.2 0.7 add_select_fusion.2
  64.6 0.7 add_select_fusion.2
  65.9 0.7 add_select_fusion.2
  67.2 0.7 add_select_fusion.2
  68.5 0.7 add_select_fusion.2
  69.8 0.7 add_select_fusion.2
  71.1 0.7 add_select_fusion.2
  72.5 0.7 add_select_fusion.2
  73.8 0.7 add_select_fusion.2
  75.1 0.7 add_select_fusion.2
  76.4 0.7 add_select_fusion.2
  77.7 0.7 add_select_fusion.2
  79.0 0.7 add_select_fusion.2
  80.3 0.7 add_select_fusion.2
  82.4 12.8 %all-gather.1 = bf16[8,2048]{1,0:T(8,128)(2,1)S(1)} all-gather(bf16[8,256]{1,0:T(8,128)(2,1)S(1)} %copy-done.8), channel_id=3, replica_groups=mesh['req'=64,'head'=8] {'head'}, dimensions={1}, use_global_device_ids=true | all-gather | bytes 36864 | tf_op jit(solution)/shard_map/all_gather | solution.py:142
  95.2 13.1 %all_gather.22 = bf16[8,16,2048]{2,1,0:T(8,128)(2,1)S(1)} all-gather(bf16[8,16,256]{2,1,0:T(8,128)(2,1)S(1)} %copy-done.6), channel_id=1, replica_groups=mesh['req'=64,'head'=8] {'head'}, dimensions={2}, use_global_device_ids=true | all-gather | bytes 589824 | tf_op jit(solution)/shard_map/all_gather | solution.py:141
  109.7 1.3 dynamic-slice
  111.0 0.7 convert_dynamic-update-slice_fusion
  111.7 146.0 %all-reduce = f32[64]{0:T(128)S(1)} all-reduce(f32[64]{0:T(128)S(1)} %convert_dynamic-update-slice_fusion), channel_id=1, replica_groups=mesh['req'=64,'head'=8] {'req'}, use_global_device_ids=true, to_apply=%add | all-reduce | flops 64 | bytes 512
  259.6 2.8 gather_fusion
  262.7 40.9 %while.25 = (s32[]{:T(128)}, f32[8,2,64,64]{3,2,1,0:T(8,128)S(1)}, f32[8,2,64,64]{3,2,1,0:T(8,128)S(1)}, f32[16,8,2,64]{3,2,1,0:T(2,128)S(1)}, f32[16,8,2,64]{3,...) while((s32[]{:T(128)}, f32[8,2,64,64]{3,2,1,0:T(8,128)S(1)}, ...), condition=%wide.region_6.7_spmd, body=%wide.region_4.6_spmd.sunk | while | flops 1052761 | bytes 1406149 | solution.py:123
  263.9 0.6 broadcast_compare_fusion.2
  274.2 0.6 broadcast_compare_fusion.2
  (285 shorter events, 64.8 us)
Async XLA Ops:
  7.2 29.2 %copy-start = (bf16[2048,64]{0,1:T(8,128)(2,1)S(1)}, bf16[2048,64]{0,1:T(8,128)(2,1)}, u32[]{:S(2)}) copy-start(bf16[2048,64]{0,1:T(8,128)(2,1)} %param.37) | copy-start | bytes 786436
  7.2 88.1 %copy-start.6 = (bf16[8,16,256]{2,1,0:T(8,128)(2,1)S(1)}, bf16[8,16,256]{2,1,0:T(8,128)(2,1)}, u32[]{:S(2)}) copy-start(bf16[8,16,256]{2,1,0:T(8,128)(2,1)} %param.23) | copy-start | bytes 196612
  7.2 75.2 %copy-start.8 = (bf16[8,256]{1,0:T(8,128)(2,1)S(1)}, bf16[8,256]{1,0:T(8,128)(2,1)}, u32[]{:S(2)}) copy-start(bf16[8,256]{1,0:T(8,128)(2,1)} %param.24) | copy-start | bytes 12292
  7.2 75.2 %copy-start.11 = (s32[8]{0:T(128)S(1)}, s32[8]{0:T(128)}, u32[]{:S(2)}) copy-start(s32[8]{0:T(128)} %param.27) | copy-start | bytes 100
  7.2 31.7 %copy-start.3 = (f32[1,2,64,64]{3,2,1,0:T(8,128)S(1)}, f32[1,2,64,64]{3,2,1,0:T(8,128)}, u32[]{:S(2)}) copy-start(f32[1,2,64,64]{3,2,1,0:T(8,128)} %param.30) | copy-start | bytes 98308
  7.2 101.5 %copy-start.7 = (bf16[64,128]{1,0:T(8,128)(2,1)S(1)}, bf16[64,128]{1,0:T(8,128)(2,1)}, u32[]{:S(2)}) copy-start(bf16[64,128]{1,0:T(8,128)(2,1)} %param.38) | copy-start | bytes 49156
  7.2 101.5 %copy-start.9 = (f32[128]{0:T(128)S(1)}, f32[128]{0:T(128)}, u32[]{:S(2)}) copy-start(f32[128]{0:T(128)} %param.39) | copy-start | bytes 1540
  7.2 252.4 %all-gather.4.cloned.1.call-start = ((), (), s32[]{:S(2)}) async-start(), calls=%async_computation | async-start | bytes 4259840 | tf_op jit(solution)/shard_map/all_gather | solution.py:234
  35.0 74.4 %copy-start.4 = (bf16[2048,128]{1,0:T(8,128)(2,1)S(1)}, bf16[2048,128]{1,0:T(8,128)(2,1)}, u32[]{:S(2)}) copy-start(bf16[2048,128]{1,0:T(8,128)(2,1)} %param.33) | copy-start | bytes 1572868
  36.4 73.3 %copy-start.12 = (f32[128]{0:T(128)S(1)}, f32[128]{0:T(128)}, u32[]{:S(2)}) copy-start(f32[128]{0:T(128)} %param.40) | copy-start | bytes 1540
  81.0 0.6 copy-start.2
  258.1 4.3 %copy-start.5 = (f32[8,2,64,64]{3,2,1,0:T(8,128)S(1)}, f32[8,2,64,64]{3,2,1,0:T(8,128)}, u32[]{:S(2)}) copy-start(f32[8,2,64,64]{3,2,1,0:T(8,128)} %param.25) | copy-start | bytes 786436
  258.6 4.0 %copy-start.13 = (s32[8]{0:T(128)S(1)}, s32[8]{0:T(128)}, u32[]{:S(2)}) copy-start(s32[8]{0:T(128)} %param.26) | copy-start | bytes 100
  262.6 42.1 %copy-start.10 = (f32[128]{0:T(128)S(1)}, f32[128]{0:T(128)}, u32[]{:S(2)}) copy-start(f32[128]{0:T(128)} %param.41) | copy-start | bytes 1540
  303.6 1.8 copy-start.1
Sparse Core Ops, SparseCore 0:
  81.8 147.0 all-gather.3
where the time goes:
time: 314 us; the launch traced here: 312 us
  blocking collectives  197 us (63%)
  other arithmetic  46.3 us (15%)
  local copies, waits for them, and re-layouts  38.6 us (12%)
  between operations  15.7 us (5%)
  matrix products  12 us (4%)
    unnamed x1, blocking collectives  146 us
    select_n x32, other arithmetic, advance_update(): return (jnp.where(valid_now[:, None, None, None], advanced, running), None)  21.6 us
    dynamic_slice x64, local copies, waits for them, and re-layouts, advance(): finished, _ = lax.scan(advance_update, initial_summary, series)  19 us
    all_gather x1, blocking collectives, widen(): lax.all_gather(following_snapshot_features, 'head', axis=2, tiled=True)  15.6 us
    all_gather x1, blocking collectives, widen(): lax.all_gather(guessed_symbol_features, 'head', axis=2, tiled=True)  13.1 us
    all_gather x1, blocking collectives, widen(): lax.all_gather(earlier_feature[:, None, :], 'head', axis=2, tiled=True)  12.8 us
    gt x16, other arithmetic, confirm_update(): approved_guesses > position  10.4 us
    dynamic_slice x48, local copies, waits for them, and re-layouts, confirm_guesses(): lax.scan(confirm_update, (initial_summary, initial_summary), series)  10.1 us
  transfers between devices with their start and end apart: 1, of which 0 were waited for; matrix products, arithmetic and copies ran while one was open for 2% of the time, Pallas kernels for 0%

commit v1 on v0

v1 whole, which is shorter than its diff:
```python
import jax
import jax.numpy as jnp
from jax import lax
from jax.experimental import pallas as pl
from jax.experimental.pallas import tpu as pltpu
from jax.sharding import PartitionSpec as P

MESH = pl.DeviceIdType.MESH
F32 = jnp.float32
BF16 = jnp.bfloat16

NX, NZ, NH = 4, 16, 8
NREQ = NX * NZ
T = 16
SPAN = 32
Q = 8
W = 2048
KS = W // NH
C = 128
HD = 64
ROWS = 72
NORM_EPS = 0.00064


def norm(o):
    return (o[0] % NX, o[1] % NZ)


def plan():
    first = [(0, 4), (0, -4), (0, 3), (0, -3), (0, 2), (0, -2), (0, 1), (0, -1)]
    second = [(-4, d) for d in (4, 3, 2, 1)] + [(4, d) for d in (-3, -2, -1)]
    stage1 = [((0, 0), norm(d)) for d in first]
    stage2 = [(norm((0, o)), norm((0, d))) for o, d in second]
    held1 = [(0, 0)] + [norm((0, -d[1])) for d in first]
    held2 = [norm((0, o - d)) for o, d in second]
    xs = [(2, 0), (1, 0), (3, 0)]
    return (
        stage1,
        stage2,
        [(o, d) for o in held1 for d in xs],
        [(o, d) for o in held2 for d in xs],
    )


STAGES = plan()
MOVES = STAGES[0] + STAGES[1] + STAGES[2] + STAGES[3]
LANDS = {norm((o[0] - d[0], o[1] - d[1])): i for i, (o, d) in enumerate(MOVES)}
PARTNERS = sorted({d for _, d in MOVES})


def split(x):
    hi = x.astype(BF16)
    return hi, (x - hi.astype(F32)).astype(BF16)


def dot(a, b):
    return jnp.dot(a, b, preferred_element_type=F32)


def dot_t(a, b):
    return lax.dot_general(a, b, (((0,), (0,)), ((), ())), preferred_element_type=F32)


def outer3(a, b):
    ah, al = split(a)
    bh, bl = split(b)
    return dot_t(ah, bh) + dot_t(ah, bl) + dot_t(al, bh)


def halves(m):
    lane = lax.broadcasted_iota(jnp.int32, (HD, C), 1)
    return jnp.where(lane < HD, m[:HD], m[HD:])


def mixes(cur, prev, mu):
    change = prev - cur
    return lambda m: (cur + change * mu[m : m + 1]).astype(BF16)


def decay_of(low, wn, we, logit):
    rank = jnp.tanh(dot(low, wn)).astype(BF16)
    return jnp.exp(-jnp.exp(logit + dot(rank, we)))


def kernel(
    approved_s, ordinal_s, restored_s, span_len_s,
    drafts_ref, earlier_ref, span_ref, span_prev_ref, mu_ref, we_ref, logit_ref, bonus_ref, gain_ref,
    state_hbm, snap_hbm, wr_hbm, wk_hbm, wv_hbm, wn_hbm,
    verified_ref, new_ref,
    state, snap, wr, wk, wv, wn,
    xs, xd, tmp, gathered, prods, rt, intra, kh, vv, kv_new,
    lsem, s_send, s_recv, d_send, d_recv, g_send, g_recv,
):
    req = lax.axis_index("req")
    me = lax.axis_index("head")
    mx, mz = req // NZ, lax.rem(req, NZ)

    def at(d):
        return lax.rem(mx + d[0], NX) * NZ + lax.rem(mz + d[1], NZ)

    local = [
        pltpu.make_async_copy(src, dst, lsem.at[i])
        for i, (src, dst) in enumerate(
            [(wk_hbm, wk), (wv_hbm, wv), (wn_hbm, wn), (snap_hbm, snap), (wr_hbm, wr), (state_hbm, state)]
        )
    ]
    for c in local:
        c.start()

    barrier = pltpu.get_barrier_semaphore()
    for k in range(1, NH):
        pl.semaphore_signal(barrier, inc=1, device_id=(req, lax.rem(me + k, NH)), device_id_type=MESH)
    for d in PARTNERS:
        pl.semaphore_signal(barrier, inc=1, device_id=(at(d), me), device_id_type=MESH)

    mine = pl.ds(pl.multiple_of(me * KS, KS), KS)
    prev8 = jnp.broadcast_to(span_prev_ref[...].astype(F32), (8, KS))
    xs[:, mine] = jnp.concatenate([prev8, span_ref[0].astype(F32)], axis=0).astype(BF16)
    for q in range(Q):
        tmp[0, pl.ds(q * T, T)] = drafts_ref[q, :, :C].astype(F32)
        tmp[1, pl.ds(q * T, T)] = drafts_ref[q, :, C:].astype(F32)
    turned = [jnp.concatenate([tmp[i, pl.ds(t, Q, stride=T)] for t in range(T)], axis=0) for i in range(2)]
    early = earlier_ref[...].astype(F32)
    xd[:, mine] = jnp.concatenate([early, jnp.concatenate(turned, axis=1)], axis=0).astype(BF16)

    pl.semaphore_wait(barrier, NH - 1 + len(PARTNERS))

    def spread(buf, send, recv, k, slot):
        ref = buf.at[:, pl.ds(pl.multiple_of(slot * KS, KS), KS)]
        return pltpu.make_async_remote_copy(
            src_ref=ref, dst_ref=ref, send_sem=send.at[k - 1], recv_sem=recv.at[k - 1],
            device_id=(req, lax.rem(me + k, NH)), device_id_type=MESH,
        )

    order = (4, 5, 3, 2, 6, 7, 1)
    for k in order:
        spread(xs, s_send, s_recv, k, me).start()
    for k in order:
        spread(xd, d_send, d_recv, k, me).start()
    for c in local[:4]:
        c.wait()
    mu = mu_ref[...]
    we = we_ref[...]
    logit = logit_ref[...]

    for k in order:
        spread(xs, s_send, s_recv, k, lax.rem(me + NH - k, NH)).wait_recv()
    both = xs[...].astype(F32)
    blend = mixes(both[8:], pltpu.roll(both, 1, axis=0)[8:], mu)
    key = dot(blend(1), wk[...])
    value = dot(blend(2), wv[...])
    decay = decay_of(blend(3), wn[...], we, logit)
    row = lax.broadcasted_iota(jnp.int32, (SPAN, C), 0)
    valid = row < span_len_s[0]
    key = jnp.where(valid, key, 0.0)
    tail = jnp.where(valid, decay, 1.0)
    for d in (1, 2, 4, 8, 16):
        tail = tail * jnp.where(row < SPAN - d, pltpu.roll(tail, SPAN - d, axis=0), 1.0)
    after = jnp.where(row < SPAN - 1, pltpu.roll(tail, SPAN - 1, axis=0), 1.0)
    whole = jnp.transpose(jnp.broadcast_to(tail[0:1], (8, C)))

    def column(m, q):
        return halves(jnp.broadcast_to(m[:, q : q + 1], (C, C)))

    def beside(ref_pair):
        return jnp.concatenate([ref_pair[0], ref_pair[1]], axis=1)

    rebuilt = column(whole, 0) * beside(snap[0]) + halves(outer3(key * after, value))
    gathered[req, pl.ds(0, HD)] = rebuilt.astype(BF16)
    place = (restored_s[0] - req * Q).astype(F32)
    gathered[req, pl.ds(HD, ROWS - HD)] = jnp.full((ROWS - HD, C), place, F32).astype(BF16)

    def move(i):
        o, d = MOVES[i]
        ref = gathered.at[at(o)]
        return pltpu.make_async_remote_copy(
            src_ref=ref, dst_ref=ref, send_sem=g_send.at[i], recv_sem=g_recv.at[i],
            device_id=(at(d), me), device_id_type=MESH,
        )

    def landed(i):
        o, d = MOVES[i]
        ref = gathered.at[at(norm((o[0] - d[0], o[1] - d[1])))]
        pltpu.make_async_remote_copy(
            src_ref=ref, dst_ref=ref, send_sem=g_send.at[i], recv_sem=g_recv.at[i],
            device_id=(at(d), me), device_id_type=MESH,
        ).wait_recv()

    n1, n2, n3, n4 = (len(s) for s in STAGES)
    for i in range(n1):
        move(i).start()
    for i in range(n1 + n2, n1 + n2 + 3):
        move(i).start()

    local[4].wait()
    local[5].wait()
    for k in order:
        spread(xd, d_send, d_recv, k, lax.rem(me + NH - k, NH)).wait_recv()
    both = xd[...].astype(F32)
    blend = mixes(both[Q:], both[:-Q], mu)
    r = dot(blend(0), wr[...]).reshape(T, Q, C)
    k = dot(blend(1), wk[...]).reshape(T, Q, C)
    v = dot(blend(2), wv[...]).reshape(T, Q, C)
    w = decay_of(blend(3), wn[...], we, logit).reshape(T, Q, C)

    for i in range(n1):
        landed(i)
    for i in range(n1, n1 + n2):
        move(i).start()
    for i in range(n1 + n2 + 3, n1 + n2 + n3):
        move(i).start()

    prods[pl.ds(0, T)] = r * bonus_ref[...].reshape(1, 1, C) * k
    run = r[1:]
    rt[pl.ds(0, Q)] = r[0]
    base = T
    bases = [0]
    for d in range(1, T):
        bases.append(base)
        prods[pl.ds(base, T - d)] = run * k[: T - d]
        base += T - d
        run = run * w[: T - d]
        rt[pl.ds(d * Q, Q)] = run[0]
        run = run[1:]
    lane_r = lax.broadcasted_iota(jnp.int32, (C, C), 0)
    lane_c = lax.broadcasted_iota(jnp.int32, (C, C), 1)
    ones = jnp.where((lane_r < HD) == (lane_c < HD), 1.0, 0.0).astype(BF16)
    ph, plo = split(prods[...].reshape(base * Q, C))
    scores = (dot(ph, ones) + dot(plo, ones)).reshape(base, Q, C)
    out = scores[0:T] * v
    acc = [out[t] for t in range(T)]
    for d in range(1, T):
        part = scores[bases[d] : bases[d] + T - d] * v[: T - d]
        for t in range(d, T):
            acc[t] = acc[t] + part[t - d]
    for t in range(T):
        intra[pl.ds(t * Q, Q)] = acc[t]

    sub = lax.broadcasted_iota(jnp.int32, (Q, C), 0)
    accepted = jnp.zeros((Q, C), jnp.int32)
    for q in range(Q):
        accepted = jnp.where(sub == q, approved_s[q], accepted)
    tail = jnp.ones((Q, C), F32)
    for t in range(T - 1, -1, -1):
        live = accepted > t
        kh[pl.ds(t * Q, Q)] = jnp.where(live, k[t], 0.0) * tail
        vv[pl.ds(t * Q, Q)] = v[t]
        tail = jnp.where(live, w[t], 1.0) * tail
    whole = jnp.transpose(tail)
    lane16 = lax.broadcasted_iota(jnp.int32, (T, C), 1)

    def per_query(ref, q):
        return ref[pl.ds(q, T, stride=Q)]

    for q in range(Q):
        kv_new[q] = halves(outer3(per_query(kh, q), per_query(vv, q)))

    for i in range(n1, n1 + n2):
        landed(i)
    for i in range(n1 + n2 + n3, len(MOVES)):
        move(i).start()
    for i in range(n1 + n2, len(MOVES)):
        landed(i)

    lane64 = lax.broadcasted_iota(jnp.int32, (HD, C), 1)
    outs = []
    for q in range(Q):
        ordinal = ordinal_s[q]
        entry = ordinal // Q
        block = gathered[entry].astype(F32)
        hit = block[HD : HD + 1] == (ordinal - entry * Q).astype(F32)
        start = jnp.where(hit, block[:HD], beside(state[q]))
        new = column(whole, q) * start + kv_new[q]
        new_ref[q, 0] = new[:, :HD]
        new_ref[q, 1] = new[:, HD:]
        rq = per_query(rt, q)
        left = jnp.concatenate([rq[:, :HD], rq[:, HD:]], axis=0)
        lh, ll = split(left)
        sh, sl = split(start)
        res = dot(lh, sh) + dot(lh, sl) + dot(ll, sh)
        outs.append(per_query(intra, q) + jnp.where(lane16 < HD, res[:T], res[T:]))
    full = jnp.concatenate(outs, axis=0)

    def head_mean(x):
        h, lo = split(x)
        return (dot(h, ones) + dot(lo, ones)) * (1.0 / HD)

    centre = full - head_mean(full)
    normed = centre * lax.rsqrt(head_mean(centre * centre) + NORM_EPS) * gain_ref[...]
    verified_ref[...] = normed.reshape(Q, T, C).astype(BF16)

    for k in order:
        spread(xs, s_send, s_recv, k, me).wait_send()
        spread(xd, d_send, d_recv, k, me).wait_send()
    for i in range(len(MOVES)):
        move(i).wait_send()


def per_device(
    drafts, earlier, state, approved, ordinals, restored, span_len, snap, span, span_prev,
    wr, wk, wv, mu, wn, we, logit, bonus, gain,
):
    smem = pl.BlockSpec(memory_space=pltpu.SMEM)
    vmem = pl.BlockSpec(memory_space=pltpu.VMEM)
    hbm = pl.BlockSpec(memory_space=pltpu.HBM)
    dma = pltpu.SemaphoreType.DMA
    n = len(MOVES)
    pairs = T * (T + 1) // 2
    return pl.pallas_call(
        kernel,
        out_shape=(
            jax.ShapeDtypeStruct((Q, T, C), BF16),
            jax.ShapeDtypeStruct((Q, 2, HD, HD), F32),
        ),
        in_specs=[smem] * 4 + [vmem] * 9 + [hbm] * 6,
        out_specs=(vmem, vmem),
        scratch_shapes=[
            pltpu.VMEM((Q, 2, HD, HD), F32),
            pltpu.VMEM((1, 2, HD, HD), F32),
            pltpu.VMEM((W, C), BF16),
            pltpu.VMEM((W, C), BF16),
            pltpu.VMEM((W, C), BF16),
            pltpu.VMEM((W, HD), BF16),
            pltpu.VMEM((8 + SPAN, W), BF16),
            pltpu.VMEM((Q + Q * T, W), BF16),
            pltpu.VMEM((2, Q * T, C), F32),
            pltpu.VMEM((NREQ, ROWS, C), BF16),
            pltpu.VMEM((pairs, Q, C), F32),
            pltpu.VMEM((T * Q, C), F32),
            pltpu.VMEM((T * Q, C), F32),
            pltpu.VMEM((T * Q, C), F32),
            pltpu.VMEM((T * Q, C), F32),
            pltpu.VMEM((Q, HD, C), F32),
            dma((6,)), dma((NH - 1,)), dma((NH - 1,)), dma((NH - 1,)), dma((NH - 1,)), dma((n,)), dma((n,)),
        ],
        compiler_params=pltpu.CompilerParams(
            collective_id=0, has_side_effects=True, vmem_limit_bytes=48 * 1024 * 1024
        ),
    )(
        approved, ordinals, restored, span_len,
        drafts, earlier, span, span_prev, mu, we, logit.reshape(1, C), bonus.reshape(1, C), gain.reshape(1, C),
        state, snap, wr, wk, wv, wn,
    )


def solution(mesh):
    in_specs = (
        P("req", None, "head"), P("req", "head"), P("req", "head", None, None), P("req"), P("req"), P("req"), P("req"),
        P("req", "head", None, None), P("req", None, "head"), P("req", "head"), P(None, "head"), P(None, "head"),
        P(None, "head"), P(), P(), P(None, "head"), P("head"), P("head"), P("head"),
    )
    out_specs = (P("req", None, "head"), P("req", "head", None, None))
    return jax.shard_map(per_device, mesh=mesh, in_specs=in_specs, out_specs=out_specs, check_vma=False)
```

time: 314 us -> 51.1 us (0.16)
  the two profiles are of different devices: /device:TPU:24 before, /device:TPU:8 now
where the time goes in v1:
time: 51.1 us; the launch traced here: 50.8 us
  Pallas kernels  42.6 us (83%)
  local copies, waits for them, and re-layouts  5.9 us (12%)
  between operations  2.22 us (4%)
    pallas_call x1, Pallas kernels, per_device(): pl.pallas_call(kernel, out_shape=(jax.ShapeDtypeStruct((Q, T, C), BF16),...  42.6 us
    unnamed x35, local copies, waits for them, and re-layouts  5.9 us

profile of v1, /device:TPU:8, one launch (start us, length us, event | category | flops | bytes accessed | tf_op | source)
XLA Modules:
  0.0 50.8 jit_solution(17201945203251917454)
XLA Ops:
  0.6 0.0 copy-start
  2.0 0.0 copy-start.4
  2.0 0.0 copy-start.5
  2.0 0.0 copy-start.6
  2.0 0.0 copy-start.7
  2.0 0.0 copy-start.8
  2.0 0.0 copy-start.9
  2.1 0.0 copy-start.10
  2.1 0.0 copy-start.11
  2.1 0.0 copy-start.12
  2.1 0.0 copy-start.13
  2.1 0.0 copy-start.14
  2.1 0.0 copy-start.15
  2.1 1.3 %copy.21.wn_hbm = bf16[2048,64]{1,0:T(8,128)(2,1)S(1)} copy(bf16[2048,64]{0,1:T(8,128)(2,1)} %param.33) | data formatting | bytes 524288 | tf_op args[14]
  3.4 0.0 copy-done
  3.5 0.0 copy-done.4
  3.5 0.0 copy-done.5
  3.5 0.0 copy-done.6
  3.5 0.0 copy-done.7
  3.5 0.0 copy-done.8
  3.5 0.0 copy-done.9
  3.5 0.0 copy-done.10
  3.5 0.0 copy-done.11
  3.5 0.0 copy-done.12
  3.5 0.0 copy-done.13
  3.6 0.0 copy-done.14
  3.6 0.0 copy-done.15
  3.6 0.0 copy-start.1
  3.6 1.0 %copy-done.1 = bf16[2048,128]{1,0:T(8,128)(2,1)S(1)} copy-done((bf16[2048,128]{1,0:T(8,128)(2,1)S(1)}, bf16[2048,128]{1,0:T(8,128)(2,1)}, u32[]{:S(2)}) %copy-start.1) | copy-done | bytes 524312
  4.6 0.0 copy-start.2
  4.6 1.0 %copy-done.2 = bf16[2048,128]{1,0:T(8,128)(2,1)S(1)} copy-done((bf16[2048,128]{1,0:T(8,128)(2,1)S(1)}, bf16[2048,128]{1,0:T(8,128)(2,1)}, u32[]{:S(2)}) %copy-start.2) | copy-done | bytes 524312
  5.7 0.0 copy-start.3
  5.7 1.0 %copy-done.3 = bf16[2048,128]{1,0:T(8,128)(2,1)S(1)} copy-done((bf16[2048,128]{1,0:T(8,128)(2,1)S(1)}, bf16[2048,128]{1,0:T(8,128)(2,1)}, u32[]{:S(2)}) %copy-start.3) | copy-done | bytes 524312
  6.7 42.6 %shard_map.194 = (bf16[8,16,128]{2,1,0:T(8,128)(2,1)S(1)}, f32[8,2,64,64]{3,2,1,0:T(8,128)S(1)}) custom-call(s32[8]{0:T(128)S(1)} %copy-done.11, s32[8]{0:T(128)S(1)} %copy-done.12, s32[1]{0:T(128)S(6)} %copy.24.restored_s, s32[1]{0:T(128)S(6)} %copy.25.span_len_s, bf16[8,16,256]{2,1,0:T(8,128)(2,1)S(1)} %copy-done.4, bf16[8,256]{1,0:T(8,128)(2,1)S(1)} %copy-done.9, ...), custom_call_target="tpu_custom_call" | custom-call | tf_op jit(solution)/shard_map/pallas_call | solution.py:309
  49.4 0.6 %copy.26 = bf16[8,16,128]{2,1,0:T(8,128)(2,1)} copy(bf16[8,16,128]{2,1,0:T(8,128)(2,1)S(1)} %get-tuple-element.4) | data formatting | bytes 65536
  50.0 0.8 %copy.27 = f32[8,2,64,64]{3,2,1,0:T(8,128)} copy(f32[8,2,64,64]{3,2,1,0:T(8,128)S(1)} %get-tuple-element.5) | data formatting | bytes 524288
Async XLA Ops:
  0.6 2.8 %copy-start = (f32[8,2,64,64]{3,2,1,0:T(8,128)S(1)}, f32[8,2,64,64]{3,2,1,0:T(8,128)}, u32[]{:S(2)}) copy-start(f32[8,2,64,64]{3,2,1,0:T(8,128)} %state_hbm.1) | copy-start | bytes 786436
  2.0 1.5 %copy-start.4 = (bf16[8,16,256]{2,1,0:T(8,128)(2,1)S(1)}, bf16[8,16,256]{2,1,0:T(8,128)(2,1)}, u32[]{:S(2)}) copy-start(bf16[8,16,256]{2,1,0:T(8,128)(2,1)} %drafts_ref.1) | copy-start | bytes 196612
  2.0 1.5 %copy-start.5 = (f32[1,2,64,64]{3,2,1,0:T(8,128)S(1)}, f32[1,2,64,64]{3,2,1,0:T(8,128)}, u32[]{:S(2)}) copy-start(f32[1,2,64,64]{3,2,1,0:T(8,128)} %snap_hbm.1) | copy-start | bytes 98308
  2.0 1.5 %copy-start.6 = (f32[4,2048]{1,0:T(4,128)S(1)}, f32[4,2048]{1,0:T(4,128)}, u32[]{:S(2)}) copy-start(f32[4,2048]{1,0:T(4,128)} %mu_ref.1) | copy-start | bytes 98308
  2.0 1.5 %copy-start.7 = (bf16[1,32,256]{2,1,0:T(8,128)(2,1)S(1)}, bf16[1,32,256]{2,1,0:T(8,128)(2,1)}, u32[]{:S(2)}) copy-start(bf16[1,32,256]{2,1,0:T(8,128)(2,1)} %span_ref.1) | copy-start | bytes 49156
  2.0 1.5 %copy-start.8 = (bf16[64,128]{1,0:T(8,128)(2,1)S(1)}, bf16[64,128]{1,0:T(8,128)(2,1)}, u32[]{:S(2)}) copy-start(bf16[64,128]{1,0:T(8,128)(2,1)} %we_ref.1) | copy-start | bytes 49156
  2.0 1.5 %copy-start.9 = (bf16[8,256]{1,0:T(8,128)(2,1)S(1)}, bf16[8,256]{1,0:T(8,128)(2,1)}, u32[]{:S(2)}) copy-start(bf16[8,256]{1,0:T(8,128)(2,1)} %earlier_ref.1) | copy-start | bytes 12292
  2.1 1.5 %copy-start.10 = (bf16[1,256]{1,0:T(2,128)(2,1)S(1)}, bf16[1,256]{1,0:T(2,128)(2,1)}, u32[]{:S(2)}) copy-start(bf16[1,256]{1,0:T(2,128)(2,1)} %span_prev_ref.1) | copy-start | bytes 1540
  2.1 1.5 %copy-start.11 = (s32[8]{0:T(128)S(1)}, s32[8]{0:T(128)}, u32[]{:S(2)}) copy-start(s32[8]{0:T(128)} %approved_s.1) | copy-start | bytes 100
  2.1 1.5 %copy-start.12 = (s32[8]{0:T(128)S(1)}, s32[8]{0:T(128)}, u32[]{:S(2)}) copy-start(s32[8]{0:T(128)} %ordinal_s.1) | copy-start | bytes 100
  2.1 1.5 %copy-start.13 = (f32[128]{0:T(128)S(1)}, f32[128]{0:T(128)}, u32[]{:S(2)}) copy-start(f32[128]{0:T(128)} %param.35) | copy-start | bytes 1540
  2.1 1.5 %copy-start.14 = (f32[128]{0:T(128)S(1)}, f32[128]{0:T(128)}, u32[]{:S(2)}) copy-start(f32[128]{0:T(128)} %param.36) | copy-start | bytes 1540
  2.1 1.5 %copy-start.15 = (f32[128]{0:T(128)S(1)}, f32[128]{0:T(128)}, u32[]{:S(2)}) copy-start(f32[128]{0:T(128)} %param.37) | copy-start | bytes 1540
  3.6 1.0 %copy-start.1 = (bf16[2048,128]{1,0:T(8,128)(2,1)S(1)}, bf16[2048,128]{1,0:T(8,128)(2,1)}, u32[]{:S(2)}) copy-start(bf16[2048,128]{1,0:T(8,128)(2,1)} %wr_hbm.1) | copy-start | bytes 1572868
  4.6 1.0 %copy-start.2 = (bf16[2048,128]{1,0:T(8,128)(2,1)S(1)}, bf16[2048,128]{1,0:T(8,128)(2,1)}, u32[]{:S(2)}) copy-start(bf16[2048,128]{1,0:T(8,128)(2,1)} %wk_hbm.1) | copy-start | bytes 1572868
  5.7 1.0 %copy-start.3 = (bf16[2048,128]{1,0:T(8,128)(2,1)S(1)}, bf16[2048,128]{1,0:T(8,128)(2,1)}, u32[]{:S(2)}) copy-start(bf16[2048,128]{1,0:T(8,128)(2,1)} %wv_hbm.1) | copy-start | bytes 1572868

commit v2 on v1

v2 whole, which is shorter than its diff:
```python
import jax
import jax.numpy as jnp
from jax import lax
from jax.experimental import pallas as pl
from jax.experimental.pallas import tpu as pltpu
from jax.sharding import PartitionSpec as P

MESH = pl.DeviceIdType.MESH
F32 = jnp.float32
BF16 = jnp.bfloat16

NX, NZ, NH = 4, 16, 8
T = 16
SPAN = 32
Q = 8
W = 2048
KS = W // NH
C = 128
HD = 64
ROWS = 72
NORM_EPS = 0.00064


FIRST = (4, -4, 3, -3, 2, -2, 1, -1)
SECOND = tuple((-4, d) for d in (4, 3, 2, 1)) + tuple((4, d) for d in (-3, -2, -1))
XS = (2, 1, 3)


def split(x):
    hi = x.astype(BF16)
    return hi, (x - hi.astype(F32)).astype(BF16)


def dot(a, b):
    return jnp.dot(a, b, preferred_element_type=F32)


def dot_t(a, b):
    return lax.dot_general(a, b, (((0,), (0,)), ((), ())), preferred_element_type=F32)


def outer3(a, b):
    ah, al = split(a)
    bh, bl = split(b)
    return dot_t(ah, bh) + dot_t(ah, bl) + dot_t(al, bh)


def halves(m):
    lane = lax.broadcasted_iota(jnp.int32, (HD, C), 1)
    return jnp.where(lane < HD, m[:HD], m[HD:])


def mixes(cur, prev, mu):
    change = prev - cur
    return lambda m: (cur + change * mu[m : m + 1]).astype(BF16)


def decay_of(low, wn, we, logit):
    low_rank = lax.dot_general(low, wn, (((1,), (1,)), ((), ())), preferred_element_type=F32)
    rank = jnp.tanh(low_rank).astype(BF16)
    return jnp.exp(-jnp.exp(logit + dot(rank, we)))


def kernel(
    approved_s, ordinal_s, restored_s, span_len_s,
    drafts_ref, earlier_ref, span_ref, span_prev_ref, mu_ref, we_ref, logit_ref, bonus_ref, gain_ref,
    state_hbm, snap_hbm, wr_hbm, wk_hbm, wv_hbm, wn_hbm,
    verified_ref, new_ref,
    state, snap, wr, wk, wv, wn,
    xs, xd, tmp, line, out_slots, in_slots, ord_v, ord_s,
    prods, rt, intra, kh, vv, kv_new, fade, lefts, base_out, base_new,
    lsem, s_send, s_recv, d_send, d_recv, z_send, z_far, z_near, z_last, x_send, x_recv, o_send, o_recv, o_sem,
):
    req = lax.axis_index("req")
    me = lax.axis_index("head")
    mx, mz = req // NZ, lax.rem(req, NZ)

    def along_z(d):
        return lax.rem(mz + (d % NZ), NZ)

    def along_x(d):
        return lax.rem(mx + d, NX)

    local = [
        pltpu.make_async_copy(src, dst, lsem.at[i])
        for i, (src, dst) in enumerate(
            [(wk_hbm, wk), (wv_hbm, wv), (wn_hbm, wn), (snap_hbm, snap), (wr_hbm, wr), (state_hbm, state)]
        )
    ]
    for c in local:
        c.start()

    barrier = pltpu.get_barrier_semaphore()
    for k in range(1, NH):
        pl.semaphore_signal(barrier, inc=1, device_id=(req, lax.rem(me + k, NH)), device_id_type=MESH)
    for d in FIRST:
        pl.semaphore_signal(barrier, inc=1, device_id=(mx * NZ + along_z(d), me), device_id_type=MESH)
    for d in XS:
        pl.semaphore_signal(barrier, inc=1, device_id=(along_x(d) * NZ + mz, me), device_id_type=MESH)

    mine = pl.ds(pl.multiple_of(me * KS, KS), KS)
    prev8 = jnp.broadcast_to(span_prev_ref[...].astype(F32), (8, KS))
    xs[:, mine] = jnp.concatenate([prev8, span_ref[0].astype(F32)], axis=0).astype(BF16)
    for q in range(Q):
        tmp[0, pl.ds(q * T, T)] = drafts_ref[q, :, :C].astype(F32)
        tmp[1, pl.ds(q * T, T)] = drafts_ref[q, :, C:].astype(F32)
    turned = [jnp.concatenate([tmp[i, pl.ds(t, Q, stride=T)] for t in range(T)], axis=0) for i in range(2)]
    early = earlier_ref[...].astype(F32)
    xd[:, mine] = jnp.concatenate([early, jnp.concatenate(turned, axis=1)], axis=0).astype(BF16)
    sub = lax.broadcasted_iota(jnp.int32, (Q, C), 0)
    accepted = jnp.zeros((Q, C), jnp.int32)
    ordinals = jnp.zeros((Q, C), jnp.int32)
    for q in range(Q):
        accepted = jnp.where(sub == q, approved_s[q], accepted)
        ordinals = jnp.where(sub == q, ordinal_s[q], ordinals)
    ord_v[mx] = ordinals

    pl.semaphore_wait(barrier, NH - 1 + len(FIRST) + len(XS))

    def spread(buf, send, recv, k, slot):
        ref = buf.at[:, pl.ds(pl.multiple_of(slot * KS, KS), KS)]
        return pltpu.make_async_remote_copy(
            src_ref=ref, dst_ref=ref, send_sem=send.at[k - 1], recv_sem=recv.at[k - 1],
            device_id=(req, lax.rem(me + k, NH)), device_id_type=MESH,
        )

    def tell(i, slot):
        ref = ord_v.at[slot]
        return pltpu.make_async_remote_copy(
            src_ref=ref, dst_ref=ref, send_sem=o_send.at[i], recv_sem=o_recv.at[i],
            device_id=(along_x(XS[i]) * NZ + mz, me), device_id_type=MESH,
        )

    order = (4, 5, 3, 2, 6, 7, 1)
    for k in order:
        spread(xs, s_send, s_recv, k, me).start()
    for i in range(len(XS)):
        tell(i, mx).start()
    for c in local[:4]:
        c.wait()
    mu = mu_ref[...]
    we = we_ref[...]
    logit = logit_ref[...]

    for k in order:
        spread(xs, s_send, s_recv, k, lax.rem(me + NH - k, NH)).wait_recv()
    for k in order:
        spread(xd, d_send, d_recv, k, me).start()
    both = xs[...].astype(F32)
    blend = mixes(both[8:], pltpu.roll(both, 1, axis=0)[8:], mu)
    key = dot(blend(1), wk[...])
    value = dot(blend(2), wv[...])
    decay = decay_of(blend(3), wn[...], we, logit)
    row = lax.broadcasted_iota(jnp.int32, (SPAN, C), 0)
    valid = row < span_len_s[0]
    key = jnp.where(valid, key, 0.0)
    tail = jnp.where(valid, decay, 1.0)
    for d in (1, 2, 4, 8, 16):
        tail = tail * jnp.where(row < SPAN - d, pltpu.roll(tail, SPAN - d, axis=0), 1.0)
    after = jnp.where(row < SPAN - 1, pltpu.roll(tail, SPAN - 1, axis=0), 1.0)
    whole = jnp.transpose(jnp.broadcast_to(tail[0:1], (8, C)))

    def column(m, q):
        return halves(jnp.broadcast_to(m[:, q : q + 1], (C, C)))

    def beside(ref_pair):
        return jnp.concatenate([ref_pair[0], ref_pair[1]], axis=1)

    rebuilt = column(whole, 0) * beside(snap[0]) + halves(outer3(key * after, value))
    line[mz, pl.ds(0, HD)] = rebuilt.astype(BF16)
    place = (restored_s[0] - req * Q).astype(F32)
    line[mz, pl.ds(HD, ROWS - HD)] = jnp.full((ROWS - HD, C), place, F32).astype(BF16)

    def hop(i, origin, d, sem):
        ref = line.at[along_z(origin)]
        return pltpu.make_async_remote_copy(
            src_ref=ref, dst_ref=ref, send_sem=z_send.at[i], recv_sem=sem,
            device_id=(mx * NZ + along_z(d), me), device_id_type=MESH,
        )

    first = [hop(i, 0, d, z_far.at[i] if i < 2 else z_near.at[i - 2]) for i, d in enumerate(FIRST)]
    second = [hop(len(FIRST) + i, o, d, z_last.at[i]) for i, (o, d) in enumerate(SECOND)]
    for c in first:
        c.start()

    local[4].wait()
    local[5].wait()
    for k in order:
        spread(xd, d_send, d_recv, k, lax.rem(me + NH - k, NH)).wait_recv()
    both = xd[...].astype(F32)
    blend = mixes(both[Q:], both[:-Q], mu)
    w = decay_of(blend(3), wn[...], we, logit).reshape(T, Q, C)
    k = dot(blend(1), wk[...]).reshape(T, Q, C)

    for i in range(2):
        hop(i, -FIRST[i], FIRST[i], z_far.at[i]).wait_recv()
    for c in second:
        c.start()

    v = dot(blend(2), wv[...]).reshape(T, Q, C)
    r = dot(blend(0), wr[...]).reshape(T, Q, C)

    prods[pl.ds(0, T)] = r * bonus_ref[...].reshape(1, 1, C) * k
    run = r[1:]
    rt[pl.ds(0, Q)] = r[0]
    base = T
    bases = [0]
    for d in range(1, T):
        bases.append(base)
        prods[pl.ds(base, T - d)] = run * k[: T - d]
        base += T - d
        run = run * w[: T - d]
        rt[pl.ds(d * Q, Q)] = run[0]
        run = run[1:]
    lane_r = lax.broadcasted_iota(jnp.int32, (C, C), 0)
    lane_c = lax.broadcasted_iota(jnp.int32, (C, C), 1)
    ones = jnp.where((lane_r < HD) == (lane_c < HD), 1.0, 0.0).astype(BF16)
    ph, plo = split(prods[...].reshape(base * Q, C))
    scores = (dot(ph, ones) + dot(plo, ones)).reshape(base, Q, C)
    out = scores[0:T] * v
    acc = [out[t] for t in range(T)]
    for d in range(1, T):
        part = scores[bases[d] : bases[d] + T - d] * v[: T - d]
        for t in range(d, T):
            acc[t] = acc[t] + part[t - d]
    for t in range(T):
        intra[pl.ds(t * Q, Q)] = acc[t]

    tail = jnp.ones((Q, C), F32)
    for t in range(T - 1, -1, -1):
        live = accepted > t
        kh[pl.ds(t * Q, Q)] = jnp.where(live, k[t], 0.0) * tail
        vv[pl.ds(t * Q, Q)] = v[t]
        tail = jnp.where(live, w[t], 1.0) * tail
    whole = jnp.transpose(tail)
    lane16 = lax.broadcasted_iota(jnp.int32, (T, C), 1)

    def pick(res):
        both = res[: 2 * T] + res[2 * T :]
        return jnp.where(lane16 < HD, both[:T], both[T:])

    for i in range(len(XS)):
        tell(i, along_x(NX - XS[i])).wait_recv()
    read = pltpu.make_async_copy(ord_v, ord_s, o_sem)
    read.start()

    for q in range(Q):
        mine_q = pl.ds(q, T, stride=Q)
        kv = halves(outer3(kh[mine_q], vv[mine_q]))
        col = column(whole, q)
        start = beside(state[q])
        kv_new[q] = kv
        fade[q] = col
        base_new[q] = col * start + kv
        rq = rt[mine_q]
        lh, ll = split(jnp.concatenate([rq[:, :HD], rq[:, HD:]], axis=0))
        left = jnp.concatenate([lh, ll], axis=0)
        lefts[q] = left
        sh, sl = split(start)
        zero = jnp.zeros((2 * T, C), F32)
        res = dot(left, sh) + jnp.concatenate([dot(lh, sl), zero], axis=0)
        base_out[q] = pick(res)
    read.wait()

    for i in range(len(FIRST) - 2):
        hop(i + 2, -FIRST[i + 2], FIRST[i + 2], z_near.at[i]).wait_recv()
    for i, (o, d) in enumerate(SECOND):
        hop(len(FIRST) + i, o - d, d, z_last.at[i]).wait_recv()

    def cross(i, slot):
        return pltpu.make_async_remote_copy(
            src_ref=out_slots.at[i], dst_ref=in_slots.at[slot], send_sem=x_send.at[i], recv_sem=x_recv.at[i],
            device_id=(along_x(XS[i]) * NZ + mz, me), device_id_type=MESH,
        )

    for i in range(len(XS)):
        for q in range(Q):
            out_slots[i, q] = line[lax.rem(ord_s[along_x(XS[i]), q, 0] // Q, NZ)]
        cross(i, mx).start()
    for q in range(Q):
        in_slots[mx, q] = line[lax.rem(ordinal_s[q] // Q, NZ)]
    for i in range(len(XS)):
        cross(i, along_x(NX - XS[i])).wait_recv()

    outs = []
    for q in range(Q):
        entry = ordinal_s[q] // Q
        block = in_slots[entry // NZ, q]
        body = block[:HD]
        hit = block[HD : HD + 1].astype(F32) == (ordinal_s[q] - entry * Q).astype(F32)
        new = jnp.where(hit, fade[q] * body.astype(F32) + kv_new[q], base_new[q])
        new_ref[q, 0] = new[:, :HD]
        new_ref[q, 1] = new[:, HD:]
        res = pick(dot(lefts[q], body))
        outs.append(intra[pl.ds(q, T, stride=Q)] + jnp.where(hit, res, base_out[q]))
    full = jnp.concatenate(outs, axis=0)

    def head_mean(x):
        h, lo = split(x)
        return (dot(h, ones) + dot(lo, ones)) * (1.0 / HD)

    centre = full - head_mean(full)
    normed = centre * lax.rsqrt(head_mean(centre * centre) + NORM_EPS) * gain_ref[...]
    verified_ref[...] = normed.reshape(Q, T, C).astype(BF16)

    for k in order:
        spread(xs, s_send, s_recv, k, me).wait_send()
        spread(xd, d_send, d_recv, k, me).wait_send()
    for c in first + second:
        c.wait_send()
    for i in range(len(XS)):
        tell(i, mx).wait_send()
        cross(i, mx).wait_send()


def per_device(
    drafts, earlier, state, approved, ordinals, restored, span_len, snap, span, span_prev,
    wr, wk, wv, mu, wn, we, logit, bonus, gain,
):
    smem = pl.BlockSpec(memory_space=pltpu.SMEM)
    vmem = pl.BlockSpec(memory_space=pltpu.VMEM)
    hbm = pl.BlockSpec(memory_space=pltpu.HBM)
    dma = pltpu.SemaphoreType.DMA
    pairs = T * (T + 1) // 2
    return pl.pallas_call(
        kernel,
        out_shape=(
            jax.ShapeDtypeStruct((Q, T, C), BF16),
            jax.ShapeDtypeStruct((Q, 2, HD, HD), F32),
        ),
        in_specs=[smem] * 4 + [vmem] * 9 + [hbm] * 6,
        out_specs=(vmem, vmem),
        scratch_shapes=[
            pltpu.VMEM((Q, 2, HD, HD), F32),
            pltpu.VMEM((1, 2, HD, HD), F32),
            pltpu.VMEM((W, C), BF16),
            pltpu.VMEM((W, C), BF16),
            pltpu.VMEM((W, C), BF16),
            pltpu.VMEM((HD, W), BF16),
            pltpu.VMEM((8 + SPAN, W), BF16),
            pltpu.VMEM((Q + Q * T, W), BF16),
            pltpu.VMEM((2, Q * T, C), F32),
            pltpu.VMEM((NZ, ROWS, C), BF16),
            pltpu.VMEM((len(XS), Q, ROWS, C), BF16),
            pltpu.VMEM((NX, Q, ROWS, C), BF16),
            pltpu.VMEM((NX, Q, C), jnp.int32),
            pltpu.SMEM((NX, Q, C), jnp.int32),
            pltpu.VMEM((pairs, Q, C), F32),
            pltpu.VMEM((T * Q, C), F32),
            pltpu.VMEM((T * Q, C), F32),
            pltpu.VMEM((T * Q, C), F32),
            pltpu.VMEM((T * Q, C), F32),
            pltpu.VMEM((Q, HD, C), F32),
            pltpu.VMEM((Q, HD, C), F32),
            pltpu.VMEM((Q, 4 * T, HD), BF16),
            pltpu.VMEM((Q, T, C), F32),
            pltpu.VMEM((Q, HD, C), F32),
            dma((6,)), dma((NH - 1,)), dma((NH - 1,)), dma((NH - 1,)), dma((NH - 1,)),
            dma((len(FIRST) + len(SECOND),)), dma((2,)), dma((len(FIRST) - 2,)), dma((len(SECOND),)),
            dma((len(XS),)), dma((len(XS),)), dma((len(XS),)), dma((len(XS),)), dma,
        ],
        compiler_params=pltpu.CompilerParams(
            collective_id=0, has_side_effects=True, vmem_limit_bytes=60 * 1024 * 1024
        ),
    )(
        approved, ordinals, restored, span_len,
        drafts, earlier, span, span_prev, mu, we, logit.reshape(1, C), bonus.reshape(1, C), gain.reshape(1, C),
        state, snap, wr, wk, wv, wn.T,
    )


def solution(mesh):
    in_specs = (
        P("req", None, "head"), P("req", "head"), P("req", "head", None, None), P("req"), P("req"), P("req"), P("req"),
        P("req", "head", None, None), P("req", None, "head"), P("req", "head"), P(None, "head"), P(None, "head"),
        P(None, "head"), P(), P(), P(None, "head"), P("head"), P("head"), P("head"),
    )
    out_specs = (P("req", None, "head"), P("req", "head", None, None))
    return jax.shard_map(per_device, mesh=mesh, in_specs=in_specs, out_specs=out_specs, check_vma=False)
```

time: 51.1 us -> 49.9 us (0.977)
  the two profiles are of different devices: /device:TPU:8 before, /device:TPU:24 now
where the time goes in v2:
time: 49.9 us; the launch traced here: 49.6 us
  Pallas kernels  44.4 us (89%)
  local copies, waits for them, and re-layouts  3.26 us (7%)
  between operations  1.94 us (4%)
    pallas_call x1, Pallas kernels, per_device(): pl.pallas_call(kernel, out_shape=(jax.ShapeDtypeStruct((Q, T, C), BF16),...  44.4 us
    unnamed x2, local copies, waits for them, and re-layouts  3.26 us

profile of v2, /device:TPU:24, one launch (start us, length us, event | category | flops | bytes accessed | tf_op | source)
XLA Modules:
  0.0 49.6 jit_solution(11755792510139004559)
XLA Ops:
  1.9 44.4 %shard_map.194 = (bf16[8,16,128]{2,1,0:T(8,128)(2,1)}, f32[8,2,64,64]{3,2,1,0:T(8,128)}) custom-call(s32[8]{0:T(128)} %approved_s.1, s32[8]{0:T(128)} %ordinal_s.1, s32[1]{0:T(128)S(6)} %copy.23.restored_s, s32[1]{0:T(128)S(6)} %copy.24.span_len_s, bf16[8,16,256]{2,1,0:T(8,128)(2,1)} %drafts_ref.1, bf16[8,256]{1,0:T(8,128)(2,1)} %earlier_ref.1, ...), custom_call_target="tpu_custom_call" | custom-call | tf_op jit(solution)/shard_map/pallas_call | solution.py:325
  46.3 1.4 %copy.25 = bf16[8,16,128]{2,1,0:T(8,128)(2,1)} copy(bf16[8,16,128]{2,1,0:T(8,128)(2,1)} %get-tuple-element.4) | data formatting | bytes 65536
  47.7 1.9 %copy.26 = f32[8,2,64,64]{3,2,1,0:T(8,128)} copy(f32[8,2,64,64]{3,2,1,0:T(8,128)} %get-tuple-element.5) | data formatting | bytes 524288

commit v3 on v2

v3 whole, which is shorter than its diff:
```python
import jax
import jax.numpy as jnp
from jax import lax
from jax.experimental import pallas as pl
from jax.experimental.pallas import tpu as pltpu
from jax.sharding import PartitionSpec as P

MESH = pl.DeviceIdType.MESH
F32 = jnp.float32
BF16 = jnp.bfloat16

NX, NZ, NH = 4, 16, 8
T = 16
SPAN = 32
Q = 8
W = 2048
KS = W // NH
C = 128
HD = 64
ROWS = 72
NORM_EPS = 0.00064


GIVEN = 19
R = 4
FIRST = tuple(d for i in range(R, 0, -1) for d in (i, -i))
SECOND = tuple((-R, d) for d in range(8 - R, 0, -1)) + tuple((R, -d) for d in range(7 - R, 0, -1))
XS = (2, 1, 3)


PARTS = ((R, 1), (0, R), (R + 1, R), (2 * R + 1, NZ - 2 * R - 1))


def slot(rel):
    return (rel + R) % NZ


def split(x):
    hi = x.astype(BF16)
    return hi, (x - hi.astype(F32)).astype(BF16)


def dot(a, b):
    return jnp.dot(a, b, preferred_element_type=F32)


def dot_t(a, b):
    return lax.dot_general(a, b, (((0,), (0,)), ((), ())), preferred_element_type=F32)


def outer3(a, b):
    ah, al = split(a)
    bh, bl = split(b)
    return dot_t(ah, bh) + dot_t(ah, bl) + dot_t(al, bh)


def halves(m):
    lane = lax.broadcasted_iota(jnp.int32, (HD, C), 1)
    return jnp.where(lane < HD, m[:HD], m[HD:])


def mixes(cur, prev, mu):
    change = prev - cur
    return lambda m: (cur + change * mu[m : m + 1]).astype(BF16)


def decay_of(low, wn, we, logit):
    low_rank = lax.dot_general(low, wn, (((1,), (1,)), ((), ())), preferred_element_type=F32)
    rank = jnp.tanh(low_rank).astype(BF16)
    return jnp.exp(-jnp.exp(logit + dot(rank, we)))


def kernel(*refs):
    given, (verified_ref, new_ref), refs = refs[:GIVEN], refs[GIVEN : GIVEN + 2], refs[GIVEN + 2 :]
    held, refs = refs[:GIVEN], refs[GIVEN:]
    (
        span_ref, span_prev_ref, drafts_ref, earlier_ref, ordinal_s, approved_s, _, _,
        mu_ref, wk, wv, wn, we_ref, logit_ref, snap, wr, state, bonus_ref, gain_ref,
    ) = held
    restored_s, span_len_s = given[6:8]
    (
    xs, xd, tmp, blocks,
    prods, rt, intra, kh, vv, kv_new, fade, lefts, base_out, base_new,
    lsem, s_send, s_recv, d_send, d_recv, z_send, z_recv, x_send, x_recv,
    ) = refs
    req = lax.axis_index("req")
    me = lax.axis_index("head")
    mx, mz = req // NZ, lax.rem(req, NZ)

    def along_z(d):
        return lax.rem(mz + (d % NZ), NZ)

    def along_x(d):
        return lax.rem(mx + d, NX)

    barrier = pltpu.get_barrier_semaphore()
    for d in FIRST:
        pl.semaphore_signal(barrier, inc=1, device_id=(mx * NZ + along_z(d), me), device_id_type=MESH)
    for k in range(1, NH):
        pl.semaphore_signal(barrier, inc=1, device_id=(req, lax.rem(me + k, NH)), device_id_type=MESH)
    for d in XS:
        pl.semaphore_signal(barrier, inc=1, device_id=(along_x(d) * NZ + mz, me), device_id_type=MESH)

    local = [pltpu.make_async_copy(src, dst, lsem.at[i]) for i, (src, dst) in enumerate(zip(given, held)) if src.shape != (1,)]
    for c in local:
        c.start()
    for c in local[:2]:
        c.wait()
    mine = pl.ds(pl.multiple_of(me * KS, KS), KS)
    prev8 = jnp.broadcast_to(span_prev_ref[...].astype(F32), (8, KS))
    xs[:, mine] = jnp.concatenate([prev8, span_ref[0].astype(F32)], axis=0).astype(BF16)

    pl.semaphore_wait(barrier, NH - 1 + len(FIRST) + len(XS))

    def spread(buf, send, recv, k, slot):
        ref = buf.at[:, pl.ds(pl.multiple_of(slot * KS, KS), KS)]
        return pltpu.make_async_remote_copy(
            src_ref=ref, dst_ref=ref, send_sem=send.at[k - 1], recv_sem=recv.at[k - 1],
            device_id=(req, lax.rem(me + k, NH)), device_id_type=MESH,
        )

    order = (4, 5, 3, 2, 6, 7, 1)
    for k in order:
        spread(xs, s_send, s_recv, k, me).start()
    for c in local[2:6]:
        c.wait()
    for q in range(Q):
        tmp[0, pl.ds(q * T, T)] = drafts_ref[q, :, :C].astype(F32)
        tmp[1, pl.ds(q * T, T)] = drafts_ref[q, :, C:].astype(F32)
    turned = [jnp.concatenate([tmp[i, pl.ds(t, Q, stride=T)] for t in range(T)], axis=0) for i in range(2)]
    early = earlier_ref[...].astype(F32)
    xd[:, mine] = jnp.concatenate([early, jnp.concatenate(turned, axis=1)], axis=0).astype(BF16)
    sub = lax.broadcasted_iota(jnp.int32, (Q, C), 0)
    accepted = jnp.zeros((Q, C), jnp.int32)
    for q in range(Q):
        accepted = jnp.where(sub == q, approved_s[q], accepted)
    for c in local[6:]:
        c.wait()
    mu = mu_ref[...]
    we = we_ref[...]
    logit = logit_ref[...]

    for k in order:
        spread(xs, s_send, s_recv, k, lax.rem(me + NH - k, NH)).wait_recv()
    for k in order:
        spread(xd, d_send, d_recv, k, me).start()
    both = xs[...].astype(F32)
    blend = mixes(both[8:], pltpu.roll(both, 1, axis=0)[8:], mu)
    key = dot(blend(1), wk[...])
    value = dot(blend(2), wv[...])
    decay = decay_of(blend(3), wn[...], we, logit)
    row = lax.broadcasted_iota(jnp.int32, (SPAN, C), 0)
    valid = row < span_len_s[0]
    key = jnp.where(valid, key, 0.0)
    tail = jnp.where(valid, decay, 1.0)
    for d in (1, 2, 4, 8, 16):
        tail = tail * jnp.where(row < SPAN - d, pltpu.roll(tail, SPAN - d, axis=0), 1.0)
    after = jnp.where(row < SPAN - 1, pltpu.roll(tail, SPAN - 1, axis=0), 1.0)
    whole = jnp.transpose(jnp.broadcast_to(tail[0:1], (8, C)))

    def column(m, q):
        return halves(jnp.broadcast_to(m[:, q : q + 1], (C, C)))

    def beside(ref_pair):
        return jnp.concatenate([ref_pair[0], ref_pair[1]], axis=1)

    rebuilt = column(whole, 0) * beside(snap[0]) + halves(outer3(key * after, value))
    blocks[0, slot(0), pl.ds(0, HD)] = rebuilt.astype(BF16)
    place = (restored_s[0] - req * Q).astype(F32)
    blocks[0, slot(0), pl.ds(HD, ROWS - HD)] = jnp.full((ROWS - HD, C), place, F32).astype(BF16)

    def hop(i, origin, d, sem):
        return pltpu.make_async_remote_copy(
            src_ref=blocks.at[0, slot(origin)], dst_ref=blocks.at[0, slot(origin - d)],
            send_sem=z_send.at[i], recv_sem=sem,
            device_id=(mx * NZ + along_z(d), me), device_id_type=MESH,
        )

    def cross(i, part):
        span = pl.ds(*PARTS[part])
        return pltpu.make_async_remote_copy(
            src_ref=blocks.at[0, span], dst_ref=blocks.at[NX - XS[i], span],
            send_sem=x_send.at[part, i], recv_sem=x_recv.at[part, i],
            device_id=(along_x(XS[i]) * NZ + mz, me), device_id_type=MESH,
        )

    def land(i, rel):
        ref = blocks.at[0, slot(rel)]
        pltpu.make_async_remote_copy(
            src_ref=ref, dst_ref=ref, send_sem=z_send.at[i], recv_sem=z_recv.at[i],
            device_id=(mx * NZ + along_z(1), me), device_id_type=MESH,
        ).wait_recv()

    n1, n2 = len(FIRST), len(SECOND)
    moves = [hop(i, 0, d, z_recv.at[i]) for i, d in enumerate(FIRST)]
    moves += [cross(i, 0) for i in range(len(XS))]
    for c in moves:
        c.start()
    for i in range(2):
        land(i, -FIRST[i])
    second = [hop(n1 + i, o, d, z_recv.at[n1 + i]) for i, (o, d) in enumerate(SECOND)]
    for c in second:
        c.start()
    for i in range(2, n1):
        land(i, -FIRST[i])
    soon = [cross(i, part) for part in (1, 2) for i in range(len(XS))]
    for c in soon:
        c.start()

    for k in order:
        spread(xd, d_send, d_recv, k, lax.rem(me + NH - k, NH)).wait_recv()
    both = xd[...].astype(F32)
    blend = mixes(both[Q:], both[:-Q], mu)
    w = decay_of(blend(3), wn[...], we, logit).reshape(T, Q, C)
    k = dot(blend(1), wk[...]).reshape(T, Q, C)

    v = dot(blend(2), wv[...]).reshape(T, Q, C)
    r = dot(blend(0), wr[...]).reshape(T, Q, C)

    prods[pl.ds(0, T)] = r * bonus_ref[...].reshape(1, 1, C) * k
    run = r[1:]
    rt[pl.ds(0, Q)] = r[0]
    base = T
    bases = [0]
    for d in range(1, T):
        bases.append(base)
        prods[pl.ds(base, T - d)] = run * k[: T - d]
        base += T - d
        run = run * w[: T - d]
        rt[pl.ds(d * Q, Q)] = run[0]
        run = run[1:]
    lane_r = lax.broadcasted_iota(jnp.int32, (C, C), 0)
    lane_c = lax.broadcasted_iota(jnp.int32, (C, C), 1)
    ones = jnp.where((lane_r < HD) == (lane_c < HD), 1.0, 0.0).astype(BF16)
    ph, plo = split(prods[...].reshape(base * Q, C))
    scores = (dot(ph, ones) + dot(plo, ones)).reshape(base, Q, C)
    out = scores[0:T] * v
    acc = [out[t] for t in range(T)]
    for d in range(1, T):
        part = scores[bases[d] : bases[d] + T - d] * v[: T - d]
        for t in range(d, T):
            acc[t] = acc[t] + part[t - d]
    for t in range(T):
        intra[pl.ds(t * Q, Q)] = acc[t]

    tail = jnp.ones((Q, C), F32)
    for t in range(T - 1, -1, -1):
        live = accepted > t
        kh[pl.ds(t * Q, Q)] = jnp.where(live, k[t], 0.0) * tail
        vv[pl.ds(t * Q, Q)] = v[t]
        tail = jnp.where(live, w[t], 1.0) * tail
    whole = jnp.transpose(tail)
    lane16 = lax.broadcasted_iota(jnp.int32, (T, C), 1)

    def pick(res):
        both = res[: 2 * T] + res[2 * T :]
        return jnp.where(lane16 < HD, both[:T], both[T:])

    for q in range(Q):
        mine_q = pl.ds(q, T, stride=Q)
        kv = halves(outer3(kh[mine_q], vv[mine_q]))
        col = column(whole, q)
        start = beside(state[q])
        kv_new[q] = kv
        fade[q] = col
        base_new[q] = col * start + kv
        rq = rt[mine_q]
        lh, ll = split(jnp.concatenate([rq[:, :HD], rq[:, HD:]], axis=0))
        left = jnp.concatenate([lh, ll], axis=0)
        lefts[q] = left
        sh, sl = split(start)
        zero = jnp.zeros((2 * T, C), F32)
        res = dot(left, sh) + jnp.concatenate([dot(lh, sl), zero], axis=0)
        base_out[q] = pick(res)
    for i in range(n2):
        land(n1 + i, SECOND[i][0] - SECOND[i][1])
    late = [cross(i, 3) for i in range(len(XS))]
    for c in late:
        c.start()
    for i in range(len(XS)):
        for part in range(len(PARTS)):
            cross(i, part).wait_recv()

    outs = []
    for q in range(Q):
        entry = ordinal_s[q] // Q
        block = blocks[lax.rem(entry // NZ + NX - mx, NX), lax.rem(entry + (NZ + R) - mz, NZ)]
        body = block[:HD]
        hit = block[HD : HD + 1].astype(F32) == (ordinal_s[q] - entry * Q).astype(F32)
        new = jnp.where(hit, fade[q] * body.astype(F32) + kv_new[q], base_new[q])
        new_ref[q, 0] = new[:, :HD]
        new_ref[q, 1] = new[:, HD:]
        res = pick(dot(lefts[q], body))
        outs.append(intra[pl.ds(q, T, stride=Q)] + jnp.where(hit, res, base_out[q]))
    full = jnp.concatenate(outs, axis=0)

    def head_mean(x):
        h, lo = split(x)
        return (dot(h, ones) + dot(lo, ones)) * (1.0 / HD)

    centre = full - head_mean(full)
    normed = centre * lax.rsqrt(head_mean(centre * centre) + NORM_EPS) * gain_ref[...]
    verified_ref[...] = normed.reshape(Q, T, C).astype(BF16)

    for k in order:
        spread(xs, s_send, s_recv, k, me).wait_send()
        spread(xd, d_send, d_recv, k, me).wait_send()
    for c in moves + second + soon + late:
        c.wait_send()


def per_device(
    drafts, earlier, state, approved, ordinals, restored, span_len, snap, span, span_prev,
    wr, wk, wv, mu, wn, we, logit, bonus, gain,
):
    given = [
        span, span_prev, drafts, earlier, ordinals, approved, restored, span_len,
        mu, wk, wv, wn.T, we, logit.reshape(1, C), snap, wr, state, bonus.reshape(1, C), gain.reshape(1, C),
    ]
    given = [x if x.size == 1 else pltpu.with_memory_space_constraint(x, pltpu.HBM) for x in given]
    held = [pltpu.SMEM(x.shape, x.dtype) if x.dtype == jnp.int32 else pltpu.VMEM(x.shape, x.dtype) for x in given]
    vmem = pl.BlockSpec(memory_space=pltpu.VMEM)
    dma = pltpu.SemaphoreType.DMA
    pairs = T * (T + 1) // 2
    return pl.pallas_call(
        kernel,
        out_shape=(
            jax.ShapeDtypeStruct((Q, T, C), BF16),
            jax.ShapeDtypeStruct((Q, 2, HD, HD), F32),
        ),
        in_specs=[pl.BlockSpec(memory_space=pltpu.SMEM if x.size == 1 else pltpu.HBM) for x in given],
        out_specs=(vmem, vmem),
        scratch_shapes=held
        + [
            pltpu.VMEM((8 + SPAN, W), BF16),
            pltpu.VMEM((Q + Q * T, W), BF16),
            pltpu.VMEM((2, Q * T, C), F32),
            pltpu.VMEM((NX, NZ, ROWS, C), BF16),
            pltpu.VMEM((pairs, Q, C), F32),
            pltpu.VMEM((T * Q, C), F32),
            pltpu.VMEM((T * Q, C), F32),
            pltpu.VMEM((T * Q, C), F32),
            pltpu.VMEM((T * Q, C), F32),
            pltpu.VMEM((Q, HD, C), F32),
            pltpu.VMEM((Q, HD, C), F32),
            pltpu.VMEM((Q, 4 * T, HD), BF16),
            pltpu.VMEM((Q, T, C), F32),
            pltpu.VMEM((Q, HD, C), F32),
            dma((GIVEN,)), dma((NH - 1,)), dma((NH - 1,)), dma((NH - 1,)), dma((NH - 1,)),
            dma((NZ - 1,)), dma((NZ - 1,)), dma((len(PARTS), len(XS))), dma((len(PARTS), len(XS))),
        ],
        compiler_params=pltpu.CompilerParams(
            collective_id=0, has_side_effects=True, vmem_limit_bytes=32 * 1024 * 1024
        ),
    )(*given)


def solution(mesh):
    in_specs = (
        P("req", None, "head"), P("req", "head"), P("req", "head", None, None), P("req"), P("req"), P("req"), P("req"),
        P("req", "head", None, None), P("req", None, "head"), P("req", "head"), P(None, "head"), P(None, "head"),
        P(None, "head"), P(), P(), P(None, "head"), P("head"), P("head"), P("head"),
    )
    out_specs = (P("req", None, "head"), P("req", "head", None, None))
    return jax.shard_map(per_device, mesh=mesh, in_specs=in_specs, out_specs=out_specs, check_vma=False)
```

time: 49.9 us -> 42.8 us (0.86)
  the two profiles are of different devices: /device:TPU:24 before, /device:TPU:8 now
where the time goes in v3:
time: 42.8 us; the launch traced here: 42.6 us
  Pallas kernels  39.3 us (92%)
  between operations  1.94 us (5%)
  local copies, waits for them, and re-layouts  1.41 us (3%)
    pallas_call x1, Pallas kernels, per_device(): pl.pallas_call(kernel, out_shape=(jax.ShapeDtypeStruct((Q, T, C), BF16),...  39.3 us
    unnamed x2, local copies, waits for them, and re-layouts  1.41 us

profile of v3, /device:TPU:8, one launch (start us, length us, event | category | flops | bytes accessed | tf_op | source)
XLA Modules:
  0.0 42.6 jit_solution(14202231045184840644)
XLA Ops:
  1.9 39.3 %shard_map.194 = (bf16[8,16,128]{2,1,0:T(8,128)(2,1)S(1)}, f32[8,2,64,64]{3,2,1,0:T(8,128)S(1)}) custom-call(bf16[1,32,256]{2,1,0:T(8,128)(2,1)} %refs_0_.1, bf16[1,256]{1,0:T(2,128)(2,1)} %refs_1_.1, bf16[8,16,256]{2,1,0:T(8,128)(2,1)} %refs_2_.1, bf16[8,256]{1,0:T(8,128)(2,1)} %refs_3_.1, s32[8]{0:T(128)} %refs_4_.1, s32[8]{0:T(128)} %refs_5_.1, ...), custom_call_target="tpu_custom_call" | custom-call | tf_op jit(solution)/shard_map/pallas_call | solution.py:325
  41.2 0.6 %copy.25 = bf16[8,16,128]{2,1,0:T(8,128)(2,1)} copy(bf16[8,16,128]{2,1,0:T(8,128)(2,1)S(1)} %get-tuple-element.4) | data formatting | bytes 65536
  41.8 0.8 %copy.26 = f32[8,2,64,64]{3,2,1,0:T(8,128)} copy(f32[8,2,64,64]{3,2,1,0:T(8,128)S(1)} %get-tuple-element.5) | data formatting | bytes 524288

commit v4 on v3

--- a/solution.py
+++ b/solution.py
@@ -28,7 +28,7 @@
 XS = (2, 1, 3)
 
 
-PARTS = ((R, 1), (0, R), (R + 1, R), (2 * R + 1, NZ - 2 * R - 1))
+PACK = Q * HD + 8
 
 
 def slot(rel):
@@ -79,9 +79,9 @@
     ) = held
     restored_s, span_len_s = given[6:8]
     (
-    xs, xd, tmp, blocks,
+    xs, xd, tmp, line, out_slots, in_slots, ord_v, ord_s,
     prods, rt, intra, kh, vv, kv_new, fade, lefts, base_out, base_new,
-    lsem, s_send, s_recv, d_send, d_recv, z_send, z_recv, x_send, x_recv,
+    lsem, s_send, s_recv, d_send, d_recv, z_send, z_recv, x_send, x_recv, o_send, o_recv, o_sem,
     ) = refs
     req = lax.axis_index("req")
     me = lax.axis_index("head")
@@ -117,6 +117,13 @@
         return pltpu.make_async_remote_copy(
             src_ref=ref, dst_ref=ref, send_sem=send.at[k - 1], recv_sem=recv.at[k - 1],
             device_id=(req, lax.rem(me + k, NH)), device_id_type=MESH,
+        )
+
+    def tell(i, source):
+        ref = ord_v.at[source]
+        return pltpu.make_async_remote_copy(
+            src_ref=ref, dst_ref=ref, send_sem=o_send.at[i], recv_sem=o_recv.at[i],
+            device_id=(along_x(XS[i]) * NZ + mz, me), device_id_type=MESH,
         )
 
     order = (4, 5, 3, 2, 6, 7, 1)
@@ -132,8 +139,13 @@
     xd[:, mine] = jnp.concatenate([early, jnp.concatenate(turned, axis=1)], axis=0).astype(BF16)
     sub = lax.broadcasted_iota(jnp.int32, (Q, C), 0)
     accepted = jnp.zeros((Q, C), jnp.int32)
+    ordinals = jnp.zeros((Q, C), jnp.int32)
     for q in range(Q):
         accepted = jnp.where(sub == q, approved_s[q], accepted)
+        ordinals = jnp.where(sub == q, ordinal_s[q], ordinals)
+    ord_v[mx] = ordinals
+    for i in range(len(XS)):
+        tell(i, mx).start()
     for c in local[6:]:
         c.wait()
     mu = mu_ref[...]
@@ -165,27 +177,25 @@
         return jnp.concatenate([ref_pair[0], ref_pair[1]], axis=1)
 
     rebuilt = column(whole, 0) * beside(snap[0]) + halves(outer3(key * after, value))
-    blocks[0, slot(0), pl.ds(0, HD)] = rebuilt.astype(BF16)
+    line[slot(0), pl.ds(0, HD)] = rebuilt.astype(BF16)
     place = (restored_s[0] - req * Q).astype(F32)
-    blocks[0, slot(0), pl.ds(HD, ROWS - HD)] = jnp.full((ROWS - HD, C), place, F32).astype(BF16)
+    line[slot(0), pl.ds(HD, ROWS - HD)] = jnp.full((ROWS - HD, C), place, F32).astype(BF16)
 
     def hop(i, origin, d, sem):
         return pltpu.make_async_remote_copy(
-            src_ref=blocks.at[0, slot(origin)], dst_ref=blocks.at[0, slot(origin - d)],
+            src_ref=line.at[slot(origin)], dst_ref=line.at[slot(origin - d)],
             send_sem=z_send.at[i], recv_sem=sem,
             device_id=(mx * NZ + along_z(d), me), device_id_type=MESH,
         )
 
-    def cross(i, part):
-        span = pl.ds(*PARTS[part])
+    def cross(i, source):
         return pltpu.make_async_remote_copy(
-            src_ref=blocks.at[0, span], dst_ref=blocks.at[NX - XS[i], span],
-            send_sem=x_send.at[part, i], recv_sem=x_recv.at[part, i],
+            src_ref=out_slots.at[i], dst_ref=in_slots.at[source], send_sem=x_send.at[i], recv_sem=x_recv.at[i],
             device_id=(along_x(XS[i]) * NZ + mz, me), device_id_type=MESH,
         )
 
     def land(i, rel):
-        ref = blocks.at[0, slot(rel)]
+        ref = line.at[slot(rel)]
         pltpu.make_async_remote_copy(
             src_ref=ref, dst_ref=ref, send_sem=z_send.at[i], recv_sem=z_recv.at[i],
             device_id=(mx * NZ + along_z(1), me), device_id_type=MESH,
@@ -193,7 +203,6 @@
 
     n1, n2 = len(FIRST), len(SECOND)
     moves = [hop(i, 0, d, z_recv.at[i]) for i, d in enumerate(FIRST)]
-    moves += [cross(i, 0) for i in range(len(XS))]
     for c in moves:
         c.start()
     for i in range(2):
@@ -201,12 +210,6 @@
     second = [hop(n1 + i, o, d, z_recv.at[n1 + i]) for i, (o, d) in enumerate(SECOND)]
     for c in second:
         c.start()
-    for i in range(2, n1):
-        land(i, -FIRST[i])
-    soon = [cross(i, part) for part in (1, 2) for i in range(len(XS))]
-    for c in soon:
-        c.start()
-
     for k in order:
         spread(xd, d_send, d_recv, k, lax.rem(me + NH - k, NH)).wait_recv()
     both = xd[...].astype(F32)
@@ -216,6 +219,12 @@
 
     v = dot(blend(2), wv[...]).reshape(T, Q, C)
     r = dot(blend(0), wr[...]).reshape(T, Q, C)
+
+    for i in range(len(XS)):
+        tell(i, along_x(NX - XS[i])).wait_recv()
+    read = pltpu.make_async_copy(ord_v, ord_s, o_sem)
+    read.start()
+    read.wait()
 
     prods[pl.ds(0, T)] = r * bonus_ref[...].reshape(1, 1, C) * k
     run = r[1:]
@@ -243,6 +252,24 @@
     for t in range(T):
         intra[pl.ds(t * Q, Q)] = acc[t]
 
+    for i in range(2, n1):
+        land(i, -FIRST[i])
+    for i in range(n2):
+        land(n1 + i, SECOND[i][0] - SECOND[i][1])
+
+    def pack(store, ordinal_of):
+        flags = []
+        for q in range(Q):
+            block = line[lax.rem(ordinal_of(q) // Q + (NZ + R) - mz, NZ)]
+            store[pl.ds(q * HD, HD)] = block[:HD]
+            flags.append(block[HD : HD + 1].astype(F32))
+        store[pl.ds(Q * HD, 8)] = jnp.concatenate(flags, axis=0).astype(BF16)
+
+    for i in range(len(XS)):
+        pack(out_slots.at[i], lambda q: ord_s[along_x(XS[i]), q, 0])
+        cross(i, mx).start()
+    pack(in_slots.at[mx], lambda q: ordinal_s[q])
+
     tail = jnp.ones((Q, C), F32)
     for t in range(T - 1, -1, -1):
         live = accepted > t
@@ -272,21 +299,16 @@
         zero = jnp.zeros((2 * T, C), F32)
         res = dot(left, sh) + jnp.concatenate([dot(lh, sl), zero], axis=0)
         base_out[q] = pick(res)
-    for i in range(n2):
-        land(n1 + i, SECOND[i][0] - SECOND[i][1])
-    late = [cross(i, 3) for i in range(len(XS))]
-    for c in late:
-        c.start()
-    for i in range(len(XS)):
-        for part in range(len(PARTS)):
-            cross(i, part).wait_recv()
+    for i in range(len(XS)):
+        cross(i, along_x(NX - XS[i])).wait_recv()
 
     outs = []
     for q in range(Q):
         entry = ordinal_s[q] // Q
-        block = blocks[lax.rem(entry // NZ + NX - mx, NX), lax.rem(entry + (NZ + R) - mz, NZ)]
-        body = block[:HD]
-        hit = block[HD : HD + 1].astype(F32) == (ordinal_s[q] - entry * Q).astype(F32)
+        source = entry // NZ
+        body = in_slots[source, pl.ds(q * HD, HD)]
+        flag = in_slots[source, pl.ds(Q * HD, 8)].astype(F32)[q : q + 1]
+        hit = flag == (ordinal_s[q] - entry * Q).astype(F32)
         new = jnp.where(hit, fade[q] * body.astype(F32) + kv_new[q], base_new[q])
         new_ref[q, 0] = new[:, :HD]
         new_ref[q, 1] = new[:, HD:]
@@ -305,8 +327,11 @@
     for k in order:
         spread(xs, s_send, s_recv, k, me).wait_send()
         spread(xd, d_send, d_recv, k, me).wait_send()
-    for c in moves + second + soon + late:
+    for c in moves + second:
         c.wait_send()
+    for i in range(len(XS)):
+        tell(i, mx).wait_send()
+        cross(i, mx).wait_send()
 
 
 def per_device(
@@ -335,7 +360,11 @@
             pltpu.VMEM((8 + SPAN, W), BF16),
             pltpu.VMEM((Q + Q * T, W), BF16),
             pltpu.VMEM((2, Q * T, C), F32),
-            pltpu.VMEM((NX, NZ, ROWS, C), BF16),
+            pltpu.VMEM((NZ, ROWS, C), BF16),
+            pltpu.VMEM((len(XS), PACK, C), BF16),
+            pltpu.VMEM((NX, PACK, C), BF16),
+            pltpu.VMEM((NX, Q, C), jnp.int32),
+            pltpu.SMEM((NX, Q, C), jnp.int32),
             pltpu.VMEM((pairs, Q, C), F32),
             pltpu.VMEM((T * Q, C), F32),
             pltpu.VMEM((T * Q, C), F32),
@@ -347,7 +376,7 @@
             pltpu.VMEM((Q, T, C), F32),
             pltpu.VMEM((Q, HD, C), F32),
             dma((GIVEN,)), dma((NH - 1,)), dma((NH - 1,)), dma((NH - 1,)), dma((NH - 1,)),
-            dma((NZ - 1,)), dma((NZ - 1,)), dma((len(PARTS), len(XS))), dma((len(PARTS), len(XS))),
+            dma((NZ - 1,)), dma((NZ - 1,)), dma((len(XS),)), dma((len(XS),)), dma((len(XS),)), dma((len(XS),)), dma,
         ],
         compiler_params=pltpu.CompilerParams(
             collective_id=0, has_side_effects=True, vmem_limit_bytes=32 * 1024 * 1024

time: 42.8 us -> 40.6 us (0.949)
  the two profiles are of different devices: /device:TPU:8 before, /device:TPU:24 now
where the time goes in v4:
time: 40.6 us; the launch traced here: 39.9 us
  Pallas kernels  36.6 us (90%)
  between operations  1.94 us (5%)
  local copies, waits for them, and re-layouts  1.41 us (3%)
    pallas_call x1, Pallas kernels, per_device(): pl.pallas_call(kernel, out_shape=(jax.ShapeDtypeStruct((Q, T, C), BF16),...  36.6 us
    unnamed x2, local copies, waits for them, and re-layouts  1.41 us

profile of v4, /device:TPU:24, one launch (start us, length us, event | category | flops | bytes accessed | tf_op | source)
XLA Modules:
  0.0 39.9 jit_solution(9664677620704405033)
XLA Ops:
  1.9 36.6 %shard_map.194 = (bf16[8,16,128]{2,1,0:T(8,128)(2,1)S(1)}, f32[8,2,64,64]{3,2,1,0:T(8,128)S(1)}) custom-call(bf16[1,32,256]{2,1,0:T(8,128)(2,1)} %refs_0_.1, bf16[1,256]{1,0:T(2,128)(2,1)} %refs_1_.1, bf16[8,16,256]{2,1,0:T(8,128)(2,1)} %refs_2_.1, bf16[8,256]{1,0:T(8,128)(2,1)} %refs_3_.1, s32[8]{0:T(128)} %refs_4_.1, s32[8]{0:T(128)} %refs_5_.1, ...), custom_call_target="tpu_custom_call" | custom-call | tf_op jit(solution)/shard_map/pallas_call | solution.py:350
  38.5 0.6 %copy.25 = bf16[8,16,128]{2,1,0:T(8,128)(2,1)} copy(bf16[8,16,128]{2,1,0:T(8,128)(2,1)S(1)} %get-tuple-element.4) | data formatting | bytes 65536
  39.2 0.8 %copy.26 = f32[8,2,64,64]{3,2,1,0:T(8,128)} copy(f32[8,2,64,64]{3,2,1,0:T(8,128)S(1)} %get-tuple-element.5) | data formatting | bytes 524288

commit v5 on v4

--- a/solution.py
+++ b/solution.py
@@ -81,7 +81,7 @@
     (
     xs, xd, tmp, line, out_slots, in_slots, ord_v, ord_s,
     prods, rt, intra, kh, vv, kv_new, fade, lefts, base_out, base_new,
-    lsem, s_send, s_recv, d_send, d_recv, z_send, z_recv, x_send, x_recv, o_send, o_recv, o_sem,
+    lsem, s_send, s_recv, d_send, d_recv, z_send, z_recv, x_send, x_recv, o_send, o_recv, o_sem, near_sem, far_sem,
     ) = refs
     req = lax.axis_index("req")
     me = lax.axis_index("head")
@@ -94,7 +94,7 @@
         return lax.rem(mx + d, NX)
 
     barrier = pltpu.get_barrier_semaphore()
-    for d in FIRST:
+    for d in (1, -1):
         pl.semaphore_signal(barrier, inc=1, device_id=(mx * NZ + along_z(d), me), device_id_type=MESH)
     for k in range(1, NH):
         pl.semaphore_signal(barrier, inc=1, device_id=(req, lax.rem(me + k, NH)), device_id_type=MESH)
@@ -110,7 +110,11 @@
     prev8 = jnp.broadcast_to(span_prev_ref[...].astype(F32), (8, KS))
     xs[:, mine] = jnp.concatenate([prev8, span_ref[0].astype(F32)], axis=0).astype(BF16)
 
-    pl.semaphore_wait(barrier, NH - 1 + len(FIRST) + len(XS))
+    def vouch(reach, sem):
+        for d in (reach, -reach):
+            pl.semaphore_signal(sem, inc=1, device_id=(mx * NZ + along_z(d), me), device_id_type=MESH)
+
+    pl.semaphore_wait(barrier, NH - 1 + 2 + len(XS))
 
     def spread(buf, send, recv, k, slot):
         ref = buf.at[:, pl.ds(pl.multiple_of(slot * KS, KS), KS)]
@@ -129,6 +133,7 @@
     order = (4, 5, 3, 2, 6, 7, 1)
     for k in order:
         spread(xs, s_send, s_recv, k, me).start()
+    vouch(1, near_sem)
     for c in local[2:6]:
         c.wait()
     for q in range(Q):
@@ -146,6 +151,8 @@
     ord_v[mx] = ordinals
     for i in range(len(XS)):
         tell(i, mx).start()
+    pl.semaphore_wait(near_sem, 2)
+    vouch(2, far_sem)
     for c in local[6:]:
         c.wait()
     mu = mu_ref[...]
@@ -202,6 +209,7 @@
         ).wait_recv()
 
     n1, n2 = len(FIRST), len(SECOND)
+    pl.semaphore_wait(far_sem, 2)
     moves = [hop(i, 0, d, z_recv.at[i]) for i, d in enumerate(FIRST)]
     for c in moves:
         c.start()
@@ -210,6 +218,30 @@
     second = [hop(n1 + i, o, d, z_recv.at[n1 + i]) for i, (o, d) in enumerate(SECOND)]
     for c in second:
         c.start()
+    for i in range(len(XS)):
+        tell(i, along_x(NX - XS[i])).wait_recv()
+    read = pltpu.make_async_copy(ord_v, ord_s, o_sem)
+    read.start()
+    read.wait()
+
+    for i in range(2, n1):
+        land(i, -FIRST[i])
+    for i in range(n2):
+        land(n1 + i, SECOND[i][0] - SECOND[i][1])
+
+    def pack(store, ordinal_of):
+        flags = []
+        for q in range(Q):
+            block = line[lax.rem(ordinal_of(q) // Q + (NZ + R) - mz, NZ)]
+            store[pl.ds(q * HD, HD)] = block[:HD]
+            flags.append(block[HD : HD + 1].astype(F32))
+        store[pl.ds(Q * HD, 8)] = jnp.concatenate(flags, axis=0).astype(BF16)
+
+    for i in range(len(XS)):
+        pack(out_slots.at[i], lambda q: ord_s[along_x(XS[i]), q, 0])
+        cross(i, mx).start()
+    pack(in_slots.at[mx], lambda q: ordinal_s[q])
+
     for k in order:
         spread(xd, d_send, d_recv, k, lax.rem(me + NH - k, NH)).wait_recv()
     both = xd[...].astype(F32)
@@ -219,12 +251,6 @@
 
     v = dot(blend(2), wv[...]).reshape(T, Q, C)
     r = dot(blend(0), wr[...]).reshape(T, Q, C)
-
-    for i in range(len(XS)):
-        tell(i, along_x(NX - XS[i])).wait_recv()
-    read = pltpu.make_async_copy(ord_v, ord_s, o_sem)
-    read.start()
-    read.wait()
 
     prods[pl.ds(0, T)] = r * bonus_ref[...].reshape(1, 1, C) * k
     run = r[1:]
@@ -251,24 +277,6 @@
             acc[t] = acc[t] + part[t - d]
     for t in range(T):
         intra[pl.ds(t * Q, Q)] = acc[t]
-
-    for i in range(2, n1):
-        land(i, -FIRST[i])
-    for i in range(n2):
-        land(n1 + i, SECOND[i][0] - SECOND[i][1])
-
-    def pack(store, ordinal_of):
-        flags = []
-        for q in range(Q):
-            block = line[lax.rem(ordinal_of(q) // Q + (NZ + R) - mz, NZ)]
-            store[pl.ds(q * HD, HD)] = block[:HD]
-            flags.append(block[HD : HD + 1].astype(F32))
-        store[pl.ds(Q * HD, 8)] = jnp.concatenate(flags, axis=0).astype(BF16)
-
-    for i in range(len(XS)):
-        pack(out_slots.at[i], lambda q: ord_s[along_x(XS[i]), q, 0])
-        cross(i, mx).start()
-    pack(in_slots.at[mx], lambda q: ordinal_s[q])
 
     tail = jnp.ones((Q, C), F32)
     for t in range(T - 1, -1, -1):
@@ -377,6 +385,7 @@
             pltpu.VMEM((Q, HD, C), F32),
             dma((GIVEN,)), dma((NH - 1,)), dma((NH - 1,)), dma((NH - 1,)), dma((NH - 1,)),
             dma((NZ - 1,)), dma((NZ - 1,)), dma((len(XS),)), dma((len(XS),)), dma((len(XS),)), dma((len(XS),)), dma,
+            pltpu.SemaphoreType.REGULAR, pltpu.SemaphoreType.REGULAR,
         ],
         compiler_params=pltpu.CompilerParams(
             collective_id=0, has_side_effects=True, vmem_limit_bytes=32 * 1024 * 1024

time: 40.6 us -> 39.9 us (0.983); the launches traced: 39.9 us -> 39.7 us
  no operation moved by 1% of the time
where the time goes in v5:
time: 39.9 us; the launch traced here: 39.7 us
  Pallas kernels  36.4 us (91%)
  between operations  1.94 us (5%)
  local copies, waits for them, and re-layouts  1.41 us (4%)
    pallas_call x1, Pallas kernels, per_device(): pl.pallas_call(kernel, out_shape=(jax.ShapeDtypeStruct((Q, T, C), BF16),...  36.4 us
    unnamed x2, local copies, waits for them, and re-layouts  1.41 us

profile of v5, /device:TPU:24, one launch (start us, length us, event | category | flops | bytes accessed | tf_op | source)
XLA Modules:
  0.0 39.7 jit_solution(12900438696368223242)
XLA Ops:
  1.9 36.4 %shard_map.194 = (bf16[8,16,128]{2,1,0:T(8,128)(2,1)S(1)}, f32[8,2,64,64]{3,2,1,0:T(8,128)S(1)}) custom-call(bf16[1,32,256]{2,1,0:T(8,128)(2,1)} %refs_0_.1, bf16[1,256]{1,0:T(2,128)(2,1)} %refs_1_.1, bf16[8,16,256]{2,1,0:T(8,128)(2,1)} %refs_2_.1, bf16[8,256]{1,0:T(8,128)(2,1)} %refs_3_.1, s32[8]{0:T(128)} %refs_4_.1, s32[8]{0:T(128)} %refs_5_.1, ...), custom_call_target="tpu_custom_call" | custom-call | tf_op jit(solution)/shard_map/pallas_call | solution.py:358
  38.3 0.6 %copy.25 = bf16[8,16,128]{2,1,0:T(8,128)(2,1)} copy(bf16[8,16,128]{2,1,0:T(8,128)(2,1)S(1)} %get-tuple-element.4) | data formatting | bytes 65536
  39.0 0.8 %copy.26 = f32[8,2,64,64]{3,2,1,0:T(8,128)} copy(f32[8,2,64,64]{3,2,1,0:T(8,128)S(1)} %get-tuple-element.5) | data formatting | bytes 524288

commit v6 on v5

--- a/solution.py
+++ b/solution.py
@@ -24,7 +24,8 @@
 GIVEN = 19
 R = 4
 FIRST = tuple(d for i in range(R, 0, -1) for d in (i, -i))
-SECOND = tuple((-R, d) for d in range(8 - R, 0, -1)) + tuple((R, -d) for d in range(7 - R, 0, -1))
+SECOND = ((-4, 4), (4, -4), (-4, 3), (4, -3), (-4, 2), (4, -2), (-4, 1), (4, -1))
+SHARE = {(-4, 4): (0, 32), (4, -4): (32, 40)}
 XS = (2, 1, 3)
 
 
@@ -189,8 +190,9 @@
     line[slot(0), pl.ds(HD, ROWS - HD)] = jnp.full((ROWS - HD, C), place, F32).astype(BF16)
 
     def hop(i, origin, d, sem):
+        part = pl.ds(*SHARE.get((origin, d), (0, ROWS)))
         return pltpu.make_async_remote_copy(
-            src_ref=line.at[slot(origin)], dst_ref=line.at[slot(origin - d)],
+            src_ref=line.at[slot(origin), part], dst_ref=line.at[slot(origin - d), part],
             send_sem=z_send.at[i], recv_sem=sem,
             device_id=(mx * NZ + along_z(d), me), device_id_type=MESH,
         )
@@ -201,8 +203,8 @@
             device_id=(along_x(XS[i]) * NZ + mz, me), device_id_type=MESH,
         )
 
-    def land(i, rel):
-        ref = line.at[slot(rel)]
+    def land(i, rel, part=(0, ROWS)):
+        ref = line.at[slot(rel), pl.ds(*part)]
         pltpu.make_async_remote_copy(
             src_ref=ref, dst_ref=ref, send_sem=z_send.at[i], recv_sem=z_recv.at[i],
             device_id=(mx * NZ + along_z(1), me), device_id_type=MESH,
@@ -227,7 +229,7 @@
     for i in range(2, n1):
         land(i, -FIRST[i])
     for i in range(n2):
-        land(n1 + i, SECOND[i][0] - SECOND[i][1])
+        land(n1 + i, SECOND[i][0] - SECOND[i][1], SHARE.get(SECOND[i], (0, ROWS)))
 
     def pack(store, ordinal_of):
         flags = []
@@ -384,7 +386,7 @@
             pltpu.VMEM((Q, T, C), F32),
             pltpu.VMEM((Q, HD, C), F32),
             dma((GIVEN,)), dma((NH - 1,)), dma((NH - 1,)), dma((NH - 1,)), dma((NH - 1,)),
-            dma((NZ - 1,)), dma((NZ - 1,)), dma((len(XS),)), dma((len(XS),)), dma((len(XS),)), dma((len(XS),)), dma,
+            dma((NZ,)), dma((NZ,)), dma((len(XS),)), dma((len(XS),)), dma((len(XS),)), dma((len(XS),)), dma,
             pltpu.SemaphoreType.REGULAR, pltpu.SemaphoreType.REGULAR,
         ],
         compiler_params=pltpu.CompilerParams(

time: 39.9 us -> 39.6 us (level)
  Pallas kernels: 36.4 us -> 36 us
where the time goes in v6:
time: 39.6 us; the launch traced here: 39.4 us
  Pallas kernels  36 us (91%)
  between operations  1.94 us (5%)
  local copies, waits for them, and re-layouts  1.41 us (4%)
    pallas_call x1, Pallas kernels, per_device(): pl.pallas_call(kernel, out_shape=(jax.ShapeDtypeStruct((Q, T, C), BF16),...  36 us
    unnamed x2, local copies, waits for them, and re-layouts  1.41 us

profile of v6, /device:TPU:24, one launch (start us, length us, event | category | flops | bytes accessed | tf_op | source)
XLA Modules:
  0.0 39.4 jit_solution(682920432827509656)
XLA Ops:
  1.9 36.0 %shard_map.194 = (bf16[8,16,128]{2,1,0:T(8,128)(2,1)S(1)}, f32[8,2,64,64]{3,2,1,0:T(8,128)S(1)}) custom-call(bf16[1,32,256]{2,1,0:T(8,128)(2,1)} %refs_0_.1, bf16[1,256]{1,0:T(2,128)(2,1)} %refs_1_.1, bf16[8,16,256]{2,1,0:T(8,128)(2,1)} %refs_2_.1, bf16[8,256]{1,0:T(8,128)(2,1)} %refs_3_.1, s32[8]{0:T(128)} %refs_4_.1, s32[8]{0:T(128)} %refs_5_.1, ...), custom_call_target="tpu_custom_call" | custom-call | tf_op jit(solution)/shard_map/pallas_call | solution.py:360
  38.0 0.6 %copy.25 = bf16[8,16,128]{2,1,0:T(8,128)(2,1)} copy(bf16[8,16,128]{2,1,0:T(8,128)(2,1)S(1)} %get-tuple-element.4) | data formatting | bytes 65536
  38.6 0.8 %copy.26 = f32[8,2,64,64]{3,2,1,0:T(8,128)} copy(f32[8,2,64,64]{3,2,1,0:T(8,128)S(1)} %get-tuple-element.5) | data formatting | bytes 524288
